TPU v7x, 512 devices: a whole 4x4x16 slice. The times are simulated.
512 devices in a mesh: blk: 16 (over y_lo, x, core), grp: 32 (over z, y_hi).
Axes of the slice: x: 4, y: 4 (y_hi: 2, y_lo: 2; y = y_hi * 2 + y_lo), z: 16, core: 2. Of those that a mesh axis runs over, the one named last changes fastest.
Arguments:
- amps: bfloat16 [4096, 8, 512], P(('blk', 'grp')), may hold values from -6 to 6
- domains: int32 [4096, 8], replicated, may hold values from 0 to 15, all different within a row
- owner: int32 [4096], replicated, may hold values from 0 to 4095, as said below
- coupling: int32 [16, 16], replicated, may hold values from 0 to 1, as said below
- integrals: bfloat16 [8192, 8192], P('blk', 'grp'), may hold values from -0.125 to 0.125
Outputs:
- residual: float32 [4096, 8192], P('blk', 'grp')
Inputs may be any that keep to these rules, and one draw needn't show every extreme that they name: `domains`: each row names 8 different pair blocks, and every block is named by some row. owner maps the occupied pairs of each group of 256 consecutive pairs one to one onto the slots of the same group. Every column of coupling holds exactly 8 ones.
All inputs are finite; a program needn't handle non-finite values.
Results may differ from a plain program's by a relative error of at most 0.0003.
Values may be sent and summed in bfloat16 or wider, within the bound.
No kernel may reach another device: no remote copies, remote signals or barrier semaphores. Data moves between devices by JAX's collectives and lax.ppermute only.
A program may use at most 64 MiB of HBM per device.

v0:
```python
import jax
import jax.numpy as jnp
from jax import lax
from jax.sharding import PartitionSpec as P


def on_device(amps, domains, owner, coupling, integrals):
    n_blk = lax.axis_size("blk")
    me_blk = lax.axis_index("blk")
    me_grp = lax.axis_index("grp")
    block_rows, col_count = integrals.shape
    col_split = block_rows // col_count
    nvb = coupling.shape[0]
    op_total = owner.shape[0]
    op_grp = op_total // n_blk
    dom_width = domains.shape[1]
    target = me_grp // col_split
    blocks = jnp.arange(nvb, dtype=jnp.int32)
    keep_col = lax.dynamic_index_in_dim(coupling, target, axis=1, keepdims=False)
    group_base = me_blk * op_grp
    own_pairs = lax.dynamic_slice_in_dim(owner, group_base, op_grp)
    local_slots = own_pairs - group_base
    group_dom = lax.dynamic_slice_in_dim(domains, group_base, op_grp)
    permuter = (local_slots[:, None] == jnp.arange(op_grp, dtype=jnp.int32)[None, :]).astype(
        jnp.float32
    )
    pair_dom = jnp.dot(
        permuter, group_dom.astype(jnp.float32), precision=lax.Precision.HIGHEST
    ).astype(jnp.int32)
    in_domain = jnp.any(pair_dom == target, axis=1).astype(jnp.float32)
    group_amps = lax.all_gather(amps, "grp", axis=0, tiled=True)
    flat_amps = group_amps.reshape(op_grp, dom_width * block_rows)
    ordered = jnp.take(flat_amps, local_slots, axis=0).reshape(op_grp, dom_width, block_rows)
    selector = (pair_dom[:, :, None] == blocks[None, None, :]) & (keep_col[None, None, :] > 0)
    tile_full = jnp.einsum(
        "pkc,pkx->pcx", selector.astype(jnp.bfloat16), ordered, preferred_element_type=jnp.float32
    )
    tile_full = tile_full.astype(jnp.bfloat16).reshape(op_grp, nvb * block_rows)
    summed = jnp.dot(
        tile_full,
        lax.all_gather(integrals, "blk", axis=0, tiled=True),
        preferred_element_type=jnp.float32,
    )
    return summed * in_domain[:, None]


def solution(mesh):
    return jax.shard_map(
        on_device,
        mesh=mesh,
        in_specs=(P(("blk", "grp"), None, None), P(), P(), P(), P("blk", "grp")),
        out_specs=P("blk", "grp"),
        check_vma=False,
    )
```

profile of v0, /device:TPU:6, one launch (start us, length us, event | category | flops | bytes accessed | tf_op | source)
XLA Modules:
  0.0 217.1 jit_solution(15730783104113241704)
XLA Ops:
  6.5 0.0 all-gather.3.cloned.1.call-start
  6.5 0.7 all-gather.3.cloned.1.call-update
  7.3 0.0 all-gather.5.cloned.1.call-start
  7.3 0.7 all-gather.5.cloned.1.call-update
  8.0 0.8 compare_and_fusion
  8.8 1.0 compare_reduce_fusion
  9.8 0.1 copy.8
  10.0 0.9 fusion.7
  10.9 153.9 %all-gather.3.cloned.1.call-done = bf16[256,8,512]{2,1,0:T(8,128)(2,1)} async-done(((bf16[8,8,512]{2,1,0:T(8,128)(2,1)}), bf16[256,8,512]{2,1,0:T(8,128)(2,1)}) %all-gather.3.cloned.1.call-update) | async-done | bytes 2097168 | tf_op jit(solution)/shard_map/all_gather | solution.py:31
  164.8 2.5 %copy.9 = bf16[32,8,8,512]{3,1,2,0:T(8,128)(2,1)S(1)} copy(bf16[32,8,8,512]{3,2,1,0:T(8,128)(2,1)} %bitcast.14) | data formatting | bytes 4194304
  167.3 3.2 %gather_fusion = bf16[256,4096]{1,0:T(8,128)(2,1)} fusion(bf16[256,4096]{1,0:T(8,128)(2,1)S(1)} %bitcast.10, s32[1024]{0:T(1024)S(1)} %pad_clamp_fusion), kind=kCustom, calls=%fused_computation | custom fusion | bytes 4195328 | tf_op jit(solution)/shard_map/jit(_take)/gather | solution.py:33
  170.4 2.5 %copy.10 = bf16[32,8,8,512]{3,2,1,0:T(8,128)(2,1)S(1)} copy(bf16[32,8,8,512]{3,1,2,0:T(8,128)(2,1)} %bitcast.12) | data formatting | bytes 4194304
  172.9 1.1 bitcast_select_fusion
  174.0 3.7 %convolution_convert_fusion = bf16[256,16,512]{2,1,0:T(8,128)(2,1)S(1)} fusion(bf16[256,8,512]{2,1,0:T(8,128)(2,1)S(1)} %bitcast_select_fusion, s32[256,8]{1,0:T(8,128)S(1)} %copy.8, pred[16]{0:T(512)(128)(4,1)S(1)} %fusion.7), kind=kOutput, calls=%fused_computation.1 | convolution fusion | flops 35717120 | bytes 6299664 | tf_op jit(solution)/shard_map/pkc,pkx->pcx/dot_general | solution.py:35
  177.8 6.3 %copy.11 = bf16[32,8,16,512]{3,1,2,0:T(8,128)(2,1)} copy(bf16[32,8,16,512]{3,2,1,0:T(8,128)(2,1)S(1)} %bitcast.11) | data formatting | bytes 8388608
  184.0 20.8 %all-gather.5.cloned.1.call-done = bf16[8192,256]{1,0:T(8,128)(2,1)} async-done(((bf16[512,256]{1,0:T(8,128)(2,1)}), bf16[8192,256]{1,0:T(8,128)(2,1)}) %all-gather.5.cloned.1.call-update) | async-done | bytes 4194320 | tf_op jit(solution)/shard_map/all_gather | solution.py:41
  204.9 5.4 %convolution_multiply_fusion = f32[256,256]{1,0:T(8,128)} fusion(bf16[256,8192]{1,0:T(8,128)(2,1)} %bitcast.13, bf16[8192,256]{1,0:T(8,128)(2,1)} %all-gather.5.cloned.1.call-done, f32[256]{0:T(256)S(1)} %convert_element_type.21), kind=kOutput, calls=%fused_computation.3 | convolution fusion | flops 1073807360 | bytes 8651776 | tf_op jit(solution)/shard_map/dot_general | solution.py:39
  (3 shorter events, 0.0 us)
Async XLA Ops:
  6.5 158.2 %all-gather.3.cloned.1.call-start = ((), (), s32[]{:S(2)}) async-start(), calls=%async_computation | async-start | bytes 2162688 | tf_op jit(solution)/shard_map/all_gather | solution.py:31
  7.3 197.6 %all-gather.5.cloned.1.call-start = ((), (), s32[]{:S(2)}) async-start(), calls=%async_computation.1 | async-start | bytes 4456448 | tf_op jit(solution)/shard_map/all_gather | solution.py:41
Sparse Core Ops, SparseCore 0:
  10.4 154.2 all-gather.2
  166.9 37.9 all-gather.4
where the time goes:
time: 220 us; the launch traced here: 217 us
  waiting for transfers between devices  176 us (80%)
  local copies, waits for them, and re-layouts  14.5 us (7%)
  between operations  13.5 us (6%)
  matrix products  10.2 us (5%)
  other arithmetic  2.75 us (1%)
    all_gather x1, waiting for transfers between devices, on_device(): group_amps = lax.all_gather(amps, 'grp', axis=0, tiled=True)  154 us
    all_gather x1, waiting for transfers between devices, on_device(): lax.all_gather(integrals, 'blk', axis=0, tiled=True)  20.8 us
    unnamed x3, local copies, waits for them, and re-layouts  11.2 us
    dot_general x1, matrix products, on_device(): jnp.dot(tile_full, lax.all_gather(integrals, 'blk', axis=0, tiled=True),...  5.42 us
  transfers between devices with their start and end apart: 2, of which 2 were waited for; matrix products, arithmetic and copies ran while one was open for 10% of the time, Pallas kernels for 0%

commit v1 on v0

v1 whole, which is shorter than its diff:
```python
import functools

import jax
import jax.numpy as jnp
from jax import lax
from jax.experimental import pallas as pl
from jax.experimental.pallas import tpu as pltpu
from jax.sharding import PartitionSpec as P

HALF_Y = 2
STRIDE = 4


def contract(
    place, coupling, dom_rows, dom_cols, owner, near, up, down, far_a, far_b, integrals,
    out, act, rows_of, tiles, blocks, sem,
):
    target, residue, group = place[0], place[1], place[2]
    n_act, pairs, depth = tiles.shape
    chunk_slots = pairs // dom_rows.shape[0]
    width = dom_rows.shape[1]
    nvb = coupling.shape[0]

    def note(c, found):
        @pl.when(coupling[c, target] > 0)
        def _():
            act[found] = c
        return found + (coupling[c, target] > 0).astype(jnp.int32)

    lax.fori_loop(0, nvb, note, jnp.int32(0))

    def fetch(i):
        start = pl.multiple_of(act[i] * depth, depth)
        return pltpu.make_async_copy(integrals.at[pl.ds(start, depth), :], blocks.at[i], sem.at[i])

    for i in range(n_act):
        fetch(i).start()

    rows = n_act * chunk_slots
    row = lax.broadcasted_iota(jnp.int32, (rows, width), 0)
    lane = lax.broadcasted_iota(jnp.int32, (rows, width), 1)
    wanted = jnp.full((rows, width), -1, jnp.int32)
    for i in range(n_act):
        wanted = jnp.where(row // chunk_slots == i, act[i], wanted)
    wanted = jnp.where(lane // (width // chunk_slots) == row % chunk_slots, wanted, -1)
    rows_of[...] = wanted

    def expand(ref, offset, z):
        pick = (dom_rows[pl.ds(z, 1), :] == rows_of[...]).astype(jnp.float32).astype(jnp.bfloat16)
        got = jnp.dot(pick, ref[pl.ds(offset, width), :], preferred_element_type=jnp.float32)
        at = pl.ds(pl.multiple_of(z * chunk_slots, chunk_slots), chunk_slots)
        for i in range(n_act):
            tiles[i, at, :] = got[i * chunk_slots : (i + 1) * chunk_slots].astype(jnp.bfloat16)

    count = near.shape[0] // width
    for ref, step in ((near, 0), (up, 1), (down, STRIDE - 1)):
        at = lax.rem(residue + step, STRIDE)
        for j in range(count):
            expand(ref, j * width, j * STRIDE + at)
    at = lax.rem(residue + 2, STRIDE)
    for j in range(count):
        ref = far_a if j < count // 2 else far_b
        expand(ref, (j % (count // 2)) * width, j * STRIDE + at)

    own = owner[pl.ds(group, 1), :] - group * pairs
    own = jnp.transpose(jnp.broadcast_to(own, (pairs, pairs)))
    slot = lax.broadcasted_iota(jnp.int32, (pairs, pairs), 1)
    inside = jnp.max((dom_cols[...] == target).astype(jnp.float32), axis=0, keepdims=True)
    order = jnp.where(own == slot, jnp.broadcast_to(inside, (pairs, pairs)), 0.0)

    total = jnp.zeros(out.shape, jnp.float32)
    for i in range(n_act):
        fetch(i).wait()
        total = total + jnp.dot(tiles[i], blocks[i], preferred_element_type=jnp.float32)
    out[...] = jnp.dot(
        order, total, precision=lax.Precision.HIGHEST, preferred_element_type=jnp.float32
    )


def on_device(amps, domains, owner, coupling, integrals):
    n_blk, n_grp = lax.axis_size("blk"), lax.axis_size("grp")
    n_z = n_grp // HALF_Y
    me_blk = lax.axis_index("blk")
    me_z = lax.axis_index("grp") // HALF_Y
    depth, cols = integrals.shape
    nvb = coupling.shape[0]
    slots, k, _ = amps.shape
    pairs = slots * n_grp
    chunk = slots * HALF_Y

    whole = lax.all_gather(integrals, "blk", axis=0, tiled=True)

    couples = [[z * HALF_Y + y for y in range(HALF_Y)] for z in range(n_z)]
    strided = [
        [(i * STRIDE + q) * HALF_Y + y for i in range(n_z // STRIDE)]
        for q in range(STRIDE)
        for y in range(HALF_Y)
    ]
    above = [((g + HALF_Y) % n_grp, g) for g in range(n_grp)]
    below = [(g, (g + HALF_Y) % n_grp) for g in range(n_grp)]
    both = lax.all_gather(amps, "grp", axis=0, tiled=True, axis_index_groups=couples)
    near = lax.all_gather(both, "grp", axis=0, tiled=True, axis_index_groups=strided)
    near = near.reshape(near.shape[0] * k, depth)
    half = near.shape[0] // 2
    up = lax.ppermute(near, "grp", above)
    down = lax.ppermute(near, "grp", below)
    far_a = lax.ppermute(up[:half], "grp", above)
    far_b = lax.ppermute(down[half:], "grp", below)

    place = jnp.stack([me_z, me_z % STRIDE, me_blk]).astype(jnp.int32)
    mine = lax.dynamic_slice_in_dim(domains, me_blk * pairs, pairs)
    dom_rows = mine.reshape(n_z, chunk * k)
    dom_cols = domains.T
    n_act = nvb // 2
    vmem = pl.BlockSpec(memory_space=pltpu.VMEM)
    smem = pl.BlockSpec(memory_space=pltpu.SMEM)
    grid_spec = pltpu.PrefetchScalarGridSpec(
        num_scalar_prefetch=1,
        grid=(1,),
        in_specs=[
            smem,
            pl.BlockSpec((n_z, chunk * k), lambda i, p: (0, 0)),
            pl.BlockSpec((k, pairs), lambda i, p: (0, p[2])),
            pl.BlockSpec((n_blk, pairs), lambda i, p: (0, 0)),
            vmem, vmem, vmem, vmem, vmem,
            pl.BlockSpec(memory_space=pltpu.HBM),
        ],
        out_specs=vmem,
        scratch_shapes=[
            pltpu.SMEM((nvb,), jnp.int32),
            pltpu.VMEM((n_act * chunk, chunk * k), jnp.int32),
            pltpu.VMEM((n_act, pairs, depth), jnp.bfloat16),
            pltpu.VMEM((n_act, depth, cols), jnp.bfloat16),
            pltpu.SemaphoreType.DMA((n_act,)),
        ],
    )
    return pl.pallas_call(
        contract,
        grid_spec=grid_spec,
        out_shape=jax.ShapeDtypeStruct((pairs, cols), jnp.float32),
        compiler_params=pltpu.CompilerParams(vmem_limit_bytes=60 * 2**20),
    )(
        place, coupling, dom_rows, dom_cols, owner.reshape(n_blk, pairs),
        near, up, down, far_a, far_b, whole,
    )


def solution(mesh):
    return jax.shard_map(
        on_device,
        mesh=mesh,
        in_specs=(P(("blk", "grp"), None, None), P(), P(), P(), P("blk", "grp")),
        out_specs=P("blk", "grp"),
        check_vma=False,
    )
```

time: 220 us -> 87.8 us (0.40); the launches traced: 217 us -> 87.5 us
  waiting for transfers between devices: 176 us -> 10.8 us
  blocking collectives: 0 us -> 37.7 us
  starting transfers between devices: 0.04 us -> 14.4 us
  local copies, waits for them, and re-layouts: 14.5 us -> 3.57 us
  matrix products: 10.2 us -> 0 us
  Pallas kernels: 0 us -> 6.78 us
    all_gather x2 -> x1, waiting for transfers between devices: 175 us -> 0.01 us  [on_device(): whole = lax.all_gather(integrals, 'blk', axis=0, tiled=True)]
    all_gather x0 -> x2, blocking collectives: none -> 37.7 us  [the longest x1 31.1 us: on_device(): lax.all_gather(both, 'grp', axis=0, tiled=True, axis_index_groups=strided)]
    ppermute x0 -> x4, starting transfers between devices: none -> 14.4 us  [the longest x1 5.29 us: on_device(): up = lax.ppermute(near, 'grp', above)]
    unnamed x3 -> x10, local copies, waits for them, and re-layouts: 11.2 us -> 0.68 us
    dot_general x3 -> x0, matrix products: 10.2 us -> none  [the longest x1 5.42 us: on_device(): jnp.dot(tile_full, lax.all_gather(integrals, 'blk', axis=0, tiled=True),...]
    ppermute x0 -> x4, waiting for transfers between devices: none -> 10.1 us  [the longest x1 6.14 us: on_device(): up = lax.ppermute(near, 'grp', above)]
    pallas_call x0 -> x1, Pallas kernels: none -> 6.78 us  [on_device(): pl.pallas_call(contract, grid_spec=grid_spec, out_shape=jax.ShapeDtypeStr...]
    gather x1 -> x0, local copies, waits for them, and re-layouts: 3.17 us -> none  [on_device(): jnp.take(flat_amps, local_slots, axis=0)]
  transfers between devices with their start and end apart: 2 -> 5, of which waited for: 2 -> 2; matrix products, arithmetic and copies ran while one was open for 10% -> 4% of each run, Pallas kernels for 0% -> 0%
where the time goes in v1:
time: 87.8 us; the launch traced here: 87.5 us
  blocking collectives  37.7 us (43%)
  starting transfers between devices  14.4 us (16%)
  between operations  13.5 us (15%)
  waiting for transfers between devices  10.8 us (12%)
  Pallas kernels  6.78 us (8%)
  local copies, waits for them, and re-layouts  3.57 us (4%)
    all_gather x1, blocking collectives, on_device(): lax.all_gather(both, 'grp', axis=0, tiled=True, axis_index_groups=strided)  31.1 us
    pallas_call x1, Pallas kernels, on_device(): pl.pallas_call(contract, grid_spec=grid_spec, out_shape=jax.ShapeDtypeStr...  6.78 us
    all_gather x1, blocking collectives, on_device(): lax.all_gather(amps, 'grp', axis=0, tiled=True, axis_index_groups=couples)  6.65 us
    ppermute x1, waiting for transfers between devices, on_device(): up = lax.ppermute(near, 'grp', above)  6.14 us
    ppermute x1, starting transfers between devices, on_device(): up = lax.ppermute(near, 'grp', above)  5.29 us
    ppermute x1, starting transfers between devices, on_device(): far_a = lax.ppermute(up[:half], 'grp', above)  5.24 us
    ppermute x1, waiting for transfers between devices, on_device(): far_b = lax.ppermute(down[half:], 'grp', below)  3.98 us
    ppermute x1, starting transfers between devices, on_device(): down = lax.ppermute(near, 'grp', below)  1.92 us
  transfers between devices with their start and end apart: 5, of which 2 were waited for; matrix products, arithmetic and copies ran while one was open for 4% of the time, Pallas kernels for 0%

profile of v1, /device:TPU:6, one launch (start us, length us, event | category | flops | bytes accessed | tf_op | source)
XLA Modules:
  0.0 87.5 jit_solution(11350707837244289388)
XLA Ops:
  6.5 0.0 all-gather.2.cloned.1.call-start
  6.5 0.7 all-gather.2.cloned.1.call-update
  7.3 6.7 %all_gather.9 = bf16[16,8,512]{2,1,0:T(8,128)(2,1)S(1)} all-gather(bf16[8,8,512]{2,1,0:T(8,128)(2,1)} %param.5), channel_id=1, replica_groups={{0,1},{2,3},{4,5},{6,7},{8,9},{10,11},{12,13},{14,15},{16,17},{18,19},{..., dimensions={0}, use_global_device_ids=true | all-gather | bytes 196608 | tf_op jit(solution)/shard_map/all_gather | solution.py:101
  13.9 31.1 %all_gather.10 = bf16[64,8,512]{2,1,0:T(8,128)(2,1)S(1)} all-gather(bf16[16,8,512]{2,1,0:T(8,128)(2,1)S(1)} %all_gather.9), channel_id=1, replica_groups={{0,8,16,24},{1,9,17,25},{2,10,18,26},{3,11,19,27},{4,12,20,28},{5,13,21..., dimensions={0}, use_global_device_ids=true | all-gather | bytes 655360 | tf_op jit(solution)/shard_map/all_gather | solution.py:102
  45.0 0.0 copy-start
  45.0 5.3 %collective-permute-start = (bf16[512,512]{1,0:T(8,128)(2,1)S(1)}, bf16[512,512]{1,0:T(8,128)(2,1)S(1)}, u32[]{:S(2)}, u32[]{:S(2)}) collective-permute-start(bf16[512,512]{1,0:T(8,128)(2,1)S(1)} %bitcast.5), channel_id=1, source_target_pairs={{2,0},{3,1},{4,2},{5,3},{6,4},{7,5},{8,6},{9,7},{10,8},{11,9},{12,... | collective-permute-start | bytes 1572872 | tf_op jit(solution)/shard_map/ppermute | solution.py:105
  50.3 1.9 %collective-permute-start.1 = (bf16[512,512]{1,0:T(8,128)(2,1)S(1)}, bf16[512,512]{1,0:T(8,128)(2,1)S(1)}, u32[]{:S(2)}, u32[]{:S(2)}) collective-permute-start(bf16[512,512]{1,0:T(8,128)(2,1)S(1)} %bitcast.6), channel_id=1, source_target_pairs={{0,2},{1,3},{2,4},{3,5},{4,6},{5,7},{6,8},{7,9},{8,10},{9,11},{10,... | collective-permute-start | bytes 1572872 | tf_op jit(solution)/shard_map/ppermute | solution.py:106
  52.2 6.1 %collective-permute-done.up = bf16[512,512]{1,0:T(8,128)(2,1)S(1)} collective-permute-done((bf16[512,512]{1,0:T(8,128)(2,1)S(1)}, bf16[512,512]{1,0:T(8,128)(2,1)S(1)}, u32[]{:S(2)}, u32[]{:S(2)}) %collective-permute-start) | collective-permute-done | bytes 524320 | tf_op jit(solution)/shard_map/ppermute | solution.py:105
  58.3 0.0 copy-start.1
  58.4 5.2 %collective-permute-start.2 = (bf16[256,512]{1,0:T(8,128)(2,1)S(1)}, bf16[256,512]{1,0:T(8,128)(2,1)S(1)}, u32[]{:S(2)}, u32[]{:S(2)}) collective-permute-start(bf16[256,512]{1,0:T(8,128)(2,1)S(1)} %slice.8), channel_id=1, source_target_pairs={{2,0},{3,1},{4,2},{5,3},{6,4},{7,5},{8,6},{9,7},{10,8},{11,9},{12,... | collective-permute-start | bytes 786440 | tf_op jit(solution)/shard_map/ppermute | solution.py:107
  63.6 0.0 collective-permute-done.1.down
  63.6 0.0 copy-start.2
  63.6 1.9 %collective-permute-start.3 = (bf16[256,512]{1,0:T(8,128)(2,1)S(1)}, bf16[256,512]{1,0:T(8,128)(2,1)S(1)}, u32[]{:S(2)}, u32[]{:S(2)}) collective-permute-start(bf16[256,512]{1,0:T(8,128)(2,1)S(1)} %slice.9), channel_id=1, source_target_pairs={{0,2},{1,3},{2,4},{3,5},{4,6},{5,7},{6,8},{7,9},{8,10},{9,11},{10,... | collective-permute-start | bytes 786440 | tf_op jit(solution)/shard_map/ppermute | solution.py:108
  65.6 0.7 constant_dynamic-slice_fusion
  66.3 0.1 copy.8
  66.4 0.7 reshape.9.dom_rows
  67.2 1.3 %reshape.10.owner = s32[16,256]{1,0:T(8,128)} reshape(s32[4096]{0:T(1024)} %param.7) | data formatting | bytes 32768 | tf_op jit(solution)/shard_map/reshape | solution.py:143
  68.5 0.7 pad_add_fusion.place
  69.1 0.0 collective-permute-done.2.far_a
  69.1 0.0 copy-start.3
  69.1 4.0 %collective-permute-done.3.far_b = bf16[256,512]{1,0:T(8,128)(2,1)S(1)} collective-permute-done((bf16[256,512]{1,0:T(8,128)(2,1)S(1)}, bf16[256,512]{1,0:T(8,128)(2,1)S(1)}, u32[]{:S(2)}, u32[]{:S(2)}) %collective-permute-start.3) | collective-permute-done | bytes 262176 | tf_op jit(solution)/shard_map/ppermute | solution.py:108
  73.1 0.0 copy-start.4
  73.1 0.0 all-gather.2.cloned.1.call-done.integrals
  73.1 0.0 copy-done
  73.1 0.0 copy-done.1
  73.1 0.0 copy-done.2
  73.1 0.0 copy-done.3
  73.2 0.7 copy-done.4
  73.8 6.8 %shard_map.55 = f32[256,256]{1,0:T(8,128)} custom-call(s32[3]{0:T(128)} %pad_add_fusion.place, s32[16,16]{1,0:T(8,128)} %coupling.1, s32[16,128]{1,0:T(8,128)} %reshape.9.dom_rows, s32[8,4096]{1,0:T(8,128)} %bitcast.8, s32[16,256]{1,0:T(8,128)} %reshape.10.owner, bf16[512,512]{1,0:T(8,128)(2,1)} %bitcast.7, bf16[512,512]{1,0:T(8,128)(2,1)} %copy-done.1, ...), custom_call_target="tpu_custom_call" | custom-call | tf_op jit(solution)/shard_map/pallas_call | solution.py:137
  (2 shorter events, 0.0 us)
Async XLA Ops:
  6.5 66.6 %all-gather.2.cloned.1.call-start = ((), (), s32[]{:S(2)}) async-start(), calls=%async_computation | async-start | bytes 4456448 | tf_op jit(solution)/shard_map/all_gather | solution.py:91
  45.0 28.2 %copy-start = (bf16[64,8,512]{2,1,0:T(8,128)(2,1)}, bf16[64,8,512]{2,1,0:T(8,128)(2,1)S(1)}, u32[]{:S(2)}) copy-start(bf16[64,8,512]{2,1,0:T(8,128)(2,1)S(1)} %all_gather.10) | copy-start | bytes 1572868
  45.0 13.4 %collective-permute-start = (bf16[512,512]{1,0:T(8,128)(2,1)S(1)}, bf16[512,512]{1,0:T(8,128)(2,1)S(1)}, u32[]{:S(2)}, u32[]{:S(2)}) collective-permute-start(bf16[512,512]{1,0:T(8,128)(2,1)S(1)} %bitcast.5), channel_id=1, source_target_pairs={{2,0},{3,1},{4,2},{5,3},{6,4},{7,5},{8,6},{9,7},{10,8},{11,9},{12,... | collective-permute-start | bytes 1572872 | tf_op jit(solution)/shard_map/ppermute | solution.py:105
  50.3 13.3 %collective-permute-start.1 = (bf16[512,512]{1,0:T(8,128)(2,1)S(1)}, bf16[512,512]{1,0:T(8,128)(2,1)S(1)}, u32[]{:S(2)}, u32[]{:S(2)}) collective-permute-start(bf16[512,512]{1,0:T(8,128)(2,1)S(1)} %bitcast.6), channel_id=1, source_target_pairs={{0,2},{1,3},{2,4},{3,5},{4,6},{5,7},{6,8},{7,9},{8,10},{9,11},{10,... | collective-permute-start | bytes 1572872 | tf_op jit(solution)/shard_map/ppermute | solution.py:106
  58.3 14.8 %copy-start.1 = (bf16[512,512]{1,0:T(8,128)(2,1)}, bf16[512,512]{1,0:T(8,128)(2,1)S(1)}, u32[]{:S(2)}) copy-start(bf16[512,512]{1,0:T(8,128)(2,1)S(1)} %collective-permute-done.up) | copy-start | bytes 1572868
  58.4 10.8 %collective-permute-start.2 = (bf16[256,512]{1,0:T(8,128)(2,1)S(1)}, bf16[256,512]{1,0:T(8,128)(2,1)S(1)}, u32[]{:S(2)}, u32[]{:S(2)}) collective-permute-start(bf16[256,512]{1,0:T(8,128)(2,1)S(1)} %slice.8), channel_id=1, source_target_pairs={{2,0},{3,1},{4,2},{5,3},{6,4},{7,5},{8,6},{9,7},{10,8},{11,9},{12,... | collective-permute-start | bytes 786440 | tf_op jit(solution)/shard_map/ppermute | solution.py:107
  63.6 9.5 %copy-start.2 = (bf16[512,512]{1,0:T(8,128)(2,1)}, bf16[512,512]{1,0:T(8,128)(2,1)S(1)}, u32[]{:S(2)}) copy-start(bf16[512,512]{1,0:T(8,128)(2,1)S(1)} %collective-permute-done.1.down) | copy-start | bytes 1572868
  63.6 9.5 %collective-permute-start.3 = (bf16[256,512]{1,0:T(8,128)(2,1)S(1)}, bf16[256,512]{1,0:T(8,128)(2,1)S(1)}, u32[]{:S(2)}, u32[]{:S(2)}) collective-permute-start(bf16[256,512]{1,0:T(8,128)(2,1)S(1)} %slice.9), channel_id=1, source_target_pairs={{0,2},{1,3},{2,4},{3,5},{4,6},{5,7},{6,8},{7,9},{8,10},{9,11},{10,... | collective-permute-start | bytes 786440 | tf_op jit(solution)/shard_map/ppermute | solution.py:108
  69.1 4.0 %copy-start.3 = (bf16[256,512]{1,0:T(8,128)(2,1)}, bf16[256,512]{1,0:T(8,128)(2,1)S(1)}, u32[]{:S(2)}) copy-start(bf16[256,512]{1,0:T(8,128)(2,1)S(1)} %collective-permute-done.2.far_a) | copy-start | bytes 786436
  73.1 0.7 copy-start.4
Sparse Core Ops, SparseCore 0:
  9.5 48.3 all-gather.1

commit v2 on v0

v2 whole, which is shorter than its diff:
```python
import jax
import jax.numpy as jnp
from jax import lax
from jax.experimental import pallas as pl
from jax.experimental.pallas import tpu as pltpu
from jax.sharding import PartitionSpec as P


HALF_Y = 2
STRIDE = 4
HEAD = 4
HEAD_MIB = 48
MIB = 2**20


EARLY = ((0, 0, 0, 4), (0, 1, 0, 4), (1, 0, 0, 4), (3, 0, 0, 4), (2, 0, 0, 4))
LATE = ((3, 1, 0, 4), (1, 1, 0, 4), (2, 1, 0, 4))


def lines_of(place, doms, k):
    width = doms.shape[1]
    lane = lax.broadcasted_iota(jnp.int32, (width, width), 1)
    other = lax.broadcasted_iota(jnp.int32, (width, width), 0)
    same = (lane // k == other // k).astype(jnp.float32).astype(jnp.bfloat16)
    table = doms[...]
    inside = (table == place[0]).astype(jnp.float32).astype(jnp.bfloat16)
    hits = jnp.dot(inside, same, preferred_element_type=jnp.float32)
    return jnp.where(hits > 0, table, -2), lax.broadcasted_iota(jnp.int32, table.shape, 0)


def expand(kinds, place, doms, pieces, tiles):
    residue, half = place[1], place[3]
    n_act, count, _ = tiles.shape
    width = doms.shape[1]
    chunk = count * width // sum(p.shape[0] for p in pieces)
    k = width // chunk
    table, table_row = lines_of(place, doms, k)
    rows = n_act * chunk
    row = lax.broadcasted_iota(jnp.int32, (rows, width), 0)
    lane = lax.broadcasted_iota(jnp.int32, (rows, width), 1)
    wanted = jnp.full((rows, width), -1, jnp.int32)
    for i in range(n_act):
        wanted = jnp.where(row // chunk == i, place[HEAD + i], wanted)
    wanted = jnp.where(lane // k == row % chunk, wanted, -1)
    per = doms.shape[0] // (HALF_Y * STRIDE)
    at = 0
    for piece, (step, across, first, z_count) in zip(pieces, kinds):
        parts = piece.shape[0] // width
        base = ((half ^ across) * STRIDE + lax.rem(residue + step, STRIDE)) * per + first * parts // z_count
        for j in range(parts):
            line = jnp.max(jnp.where(table_row == base + j, table, -2), axis=0, keepdims=True)
            pick = (line == wanted).astype(jnp.float32).astype(jnp.bfloat16)
            got = jnp.dot(pick, piece[pl.ds(j * width, width), :], preferred_element_type=jnp.float32)
            for i in range(n_act):
                tiles[i, at : at + chunk, :] = got[i * chunk : (i + 1) * chunk].astype(jnp.bfloat16)
            at += chunk


def head_kernel(place, doms, *refs):
    pieces, (integrals, part, blocks, tiles, sem) = refs[: len(EARLY)], refs[len(EARLY) :]
    n_act, depth, _ = blocks.shape

    def fetch(i):
        start = pl.multiple_of(place[HEAD + i] * depth, depth)
        return pltpu.make_async_copy(integrals.at[pl.ds(start, depth), :], blocks.at[i], sem.at[i])

    for i in range(n_act):
        fetch(i).start()
    expand(EARLY, place, doms, pieces, tiles)
    total = jnp.zeros(part.shape, jnp.float32)
    for i in range(n_act):
        fetch(i).wait()
        total = total + jnp.dot(tiles[i], blocks[i], preferred_element_type=jnp.float32)
    part[...] = total


def finish_kernel(place, doms, owner, part, blocks, *refs):
    pieces, out, tiles = refs[:-2], refs[-2], refs[-1]
    residue, group, half = place[1], place[2], place[3]
    expand(LATE, place, doms, pieces, tiles)
    pairs = out.shape[0]
    per_z = pairs // sum(c for *_, c in EARLY + LATE)
    at = lax.broadcasted_iota(jnp.int32, (1, pairs), 1)
    slot = jnp.zeros((1, pairs), jnp.int32)
    low = 0
    for step, across, first, z_count in EARLY + LATE:
        inner = at - low
        z = (first + inner // per_z) * STRIDE + lax.rem(residue + step, STRIDE)
        here = (z * HALF_Y + (half ^ across)) * per_z + inner % per_z
        slot = jnp.where(at >= low, here, slot)
        low += z_count * per_z
    own = owner[pl.ds(group, 1), :] - group * pairs
    own = jnp.transpose(jnp.broadcast_to(own, (pairs, pairs)))
    order = (own == slot).astype(jnp.float32)
    total = jnp.zeros((tiles.shape[1], out.shape[1]), jnp.float32)
    for i in range(tiles.shape[0]):
        total = total + jnp.dot(tiles[i], blocks[i], preferred_element_type=jnp.float32)
    out[...] = jnp.dot(
        order,
        jnp.concatenate([part[...], total], axis=0),
        precision=lax.Precision.HIGHEST,
        preferred_element_type=jnp.float32,
    )


def on_device(amps, domains, owner, coupling, integrals):
    n_blk, n_grp = lax.axis_size("blk"), lax.axis_size("grp")
    n_z = n_grp // HALF_Y
    me_blk, me_grp = lax.axis_index("blk"), lax.axis_index("grp")
    me_z = me_grp // HALF_Y
    depth, cols = integrals.shape
    nvb = coupling.shape[0]
    n_act = nvb // 2
    slots, k, _ = amps.shape
    pairs = slots * n_grp

    whole = lax.all_gather(integrals, "blk", axis=0, tiled=True)

    strided = [
        [(i * STRIDE + q) * HALF_Y + y for i in range(n_z // STRIDE)]
        for q in range(STRIDE)
        for y in range(HALF_Y)
    ]

    def send(x, hops):
        return lax.ppermute(x, "grp", [(g, (g + hops * HALF_Y) % n_grp) for g in range(n_grp)])

    near = lax.all_gather(amps, "grp", axis=0, tiled=True, axis_index_groups=strided)
    near = near.reshape(near.shape[0] * k, depth)
    near_x = lax.ppermute(near, "grp", [(g, g ^ 1) for g in range(n_grp)])
    up = send(near, -1)
    down = send(near, 1)

    keep = lax.dynamic_index_in_dim(coupling, me_z, axis=1, keepdims=False) > 0
    numbers = jnp.arange(nvb, dtype=jnp.int32)
    before = jnp.sum((numbers[None, :] < numbers[:, None]) & keep[None, :], axis=1)
    chosen = keep[None, :] & (before[None, :] == jnp.arange(n_act)[:, None])
    act = jnp.sum(jnp.where(chosen, numbers[None, :], 0), axis=1)
    head = jnp.stack([me_z, me_z % STRIDE, me_blk, me_grp % HALF_Y])
    place = jnp.concatenate([head, act]).astype(jnp.int32)
    mine = lax.dynamic_slice_in_dim(domains, me_blk * pairs, pairs)
    mine = mine.reshape(n_z // STRIDE, STRIDE, HALF_Y, slots * k)
    doms = jnp.transpose(mine, (2, 1, 0, 3)).reshape(-1, 2 * slots * k)
    owners = owner.reshape(n_blk, pairs)
    ready, place, doms, owners = lax.optimization_barrier((up, place, doms, owners))
    far = send(ready, -1)
    down_x = send(near_x, 1)
    up_x = send(near_x, -1)
    far_x = send(down_x, 1)
    vmem = pl.BlockSpec(memory_space=pltpu.VMEM)
    smem = pl.BlockSpec(memory_space=pltpu.SMEM)

    def cost(flops):
        return pl.CostEstimate(flops=flops, bytes_accessed=2 * MIB, transcendentals=0)

    pieces = (near, near_x, up, down, far)
    rows = sum(p.shape[0] for p in pieces) // k
    part, blocks = pl.pallas_call(
        head_kernel,
        in_specs=[smem] + [vmem] * (1 + len(pieces)) + [pl.BlockSpec(memory_space=pl.ANY)],
        out_specs=(vmem, vmem),
        out_shape=(
            jax.ShapeDtypeStruct((rows, cols), jnp.float32),
            jax.ShapeDtypeStruct((n_act, depth, cols), jnp.bfloat16),
        ),
        scratch_shapes=[
            pltpu.VMEM((n_act, rows, depth), jnp.bfloat16),
            pltpu.SemaphoreType.DMA((n_act,)),
        ],
        compiler_params=pltpu.CompilerParams(vmem_limit_bytes=HEAD_MIB * MIB),
        cost_estimate=cost(2**29),
    )(place, doms, *pieces, whole)
    pieces = (down_x, up_x, far_x)
    return pl.pallas_call(
        finish_kernel,
        in_specs=[smem] + [vmem] * (4 + len(pieces)),
        out_specs=vmem,
        out_shape=jax.ShapeDtypeStruct((pairs, cols), jnp.float32),
        scratch_shapes=[pltpu.VMEM((n_act, pairs - rows, depth), jnp.bfloat16)],
        compiler_params=pltpu.CompilerParams(vmem_limit_bytes=16 * MIB),
        cost_estimate=cost(2**29),
    )(place, doms, owners, part, blocks, *pieces)


def solution(mesh):
    return jax.shard_map(
        on_device,
        mesh=mesh,
        in_specs=(P(("blk", "grp"), None, None), P(), P(), P(), P("blk", "grp")),
        out_specs=P("blk", "grp"),
        check_vma=False,
    )
```

time: 220 us -> 81 us (0.37); the launches traced: 217 us -> 80.5 us
  waiting for transfers between devices: 176 us -> 7.61 us
  blocking collectives: 0 us -> 27.1 us
  starting transfers between devices: 0.04 us -> 23.9 us
  local copies, waits for them, and re-layouts: 14.5 us -> 1.14 us
  matrix products: 10.2 us -> 0 us
  Pallas kernels: 0 us -> 6.13 us
    all_gather x2 -> x1, waiting for transfers between devices: 175 us -> 0.02 us  [on_device(): whole = lax.all_gather(integrals, 'blk', axis=0, tiled=True)]
    all_gather x0 -> x1, blocking collectives: none -> 27.1 us  [on_device(): lax.all_gather(amps, 'grp', axis=0, tiled=True, axis_index_groups=strided)]
    ppermute x0 -> x7, starting transfers between devices: none -> 23.9 us  [the longest x6 18.8 us: send(): lax.ppermute(x, 'grp', [(g, (g + hops * HALF_Y) % n_grp) for g in range(n...]
    unnamed x3 -> x2, local copies, waits for them, and re-layouts: 11.2 us -> 0.01 us
    dot_general x3 -> x0, matrix products: 10.2 us -> none  [the longest x1 5.42 us: on_device(): jnp.dot(tile_full, lax.all_gather(integrals, 'blk', axis=0, tiled=True),...]
    ppermute x0 -> x7, waiting for transfers between devices: none -> 6.88 us  [the longest x1 3.86 us: on_device(): near_x = lax.ppermute(near, 'grp', [(g, g ^ 1) for g in range(n_grp)])]
    pallas_call x0 -> x2, Pallas kernels: none -> 6.13 us  [the longest x1 3.26 us: on_device(): pl.pallas_call(head_kernel, in_specs=[smem] + [vmem] * (1 + len(pieces))...]
    gather x1 -> x0, local copies, waits for them, and re-layouts: 3.17 us -> none  [on_device(): jnp.take(flat_amps, local_slots, axis=0)]
  transfers between devices with their start and end apart: 2 -> 8, of which waited for: 2 -> 2; matrix products, arithmetic and copies ran while one was open for 10% -> 3% of each run, Pallas kernels for 0% -> 4%
where the time goes in v2:
time: 81 us; the launch traced here: 80.5 us
  blocking collectives  27.1 us (33%)
  starting transfers between devices  23.9 us (30%)
  between operations  13.6 us (17%)
  waiting for transfers between devices  7.61 us (9%)
  Pallas kernels  6.13 us (8%)
  local copies, waits for them, and re-layouts  1.14 us (1%)
  other arithmetic  1.12 us (1%)
    all_gather x1, blocking collectives, on_device(): lax.all_gather(amps, 'grp', axis=0, tiled=True, axis_index_groups=strided)  27.1 us
    ppermute x6, starting transfers between devices, send(): lax.ppermute(x, 'grp', [(g, (g + hops * HALF_Y) % n_grp) for g in range(n...  18.8 us
    ppermute x1, starting transfers between devices, on_device(): near_x = lax.ppermute(near, 'grp', [(g, g ^ 1) for g in range(n_grp)])  5.09 us
    ppermute x1, waiting for transfers between devices, on_device(): near_x = lax.ppermute(near, 'grp', [(g, g ^ 1) for g in range(n_grp)])  3.86 us
    pallas_call x1, Pallas kernels, on_device(): pl.pallas_call(head_kernel, in_specs=[smem] + [vmem] * (1 + len(pieces))...  3.26 us
    ppermute x6, waiting for transfers between devices, send(): lax.ppermute(x, 'grp', [(g, (g + hops * HALF_Y) % n_grp) for g in range(n...  3.02 us
    pallas_call x1, Pallas kernels, on_device(): pl.pallas_call(finish_kernel, in_specs=[smem] + [vmem] * (4 + len(pieces)...  2.87 us
  transfers between devices with their start and end apart: 8, of which 2 were waited for; matrix products, arithmetic and copies ran while one was open for 3% of the time, Pallas kernels for 4%

profile of v2, /device:TPU:6, one launch (start us, length us, event | category | flops | bytes accessed | tf_op | source)
XLA Modules:
  0.0 80.5 jit_solution(15346982104935714070)
XLA Ops:
  6.5 0.0 copy-start
  6.5 0.0 all-gather.2.cloned.1.call-start
  6.5 0.7 all-gather.2.cloned.1.call-update
  7.3 27.1 %all_gather.6 = bf16[32,8,512]{2,1,0:T(8,128)(2,1)S(1)} all-gather(bf16[8,8,512]{2,1,0:T(8,128)(2,1)} %param.5), channel_id=1, replica_groups={{0,8,16,24},{1,9,17,25},{2,10,18,26},{3,11,19,27},{4,12,20,28},{5,13,21..., dimensions={0}, use_global_device_ids=true | all-gather | bytes 327680 | tf_op jit(solution)/shard_map/all_gather | solution.py:128
  34.4 5.1 %collective-permute-start.1 = (bf16[256,512]{1,0:T(8,128)(2,1)S(1)}, bf16[256,512]{1,0:T(8,128)(2,1)S(1)}, u32[]{:S(2)}, u32[]{:S(2)}) collective-permute-start(bf16[256,512]{1,0:T(8,128)(2,1)S(1)} %bitcast.6), channel_id=1, source_target_pairs={{0,1},{1,0},{2,3},{3,2},{4,5},{5,4},{6,7},{7,6},{8,9},{9,8},{10,11... | collective-permute-start | bytes 786440 | tf_op jit(solution)/shard_map/ppermute | solution.py:130
  39.5 4.0 %collective-permute-start = (bf16[256,512]{1,0:T(8,128)(2,1)S(1)}, bf16[256,512]{1,0:T(8,128)(2,1)S(1)}, u32[]{:S(2)}, u32[]{:S(2)}) collective-permute-start(bf16[256,512]{1,0:T(8,128)(2,1)S(1)} %bitcast.7), channel_id=1, source_target_pairs={{0,30},{1,31},{2,0},{3,1},{4,2},{5,3},{6,4},{7,5},{8,6},{9,7},{10,... | collective-permute-start | bytes 786440 | tf_op jit(solution)/shard_map/ppermute | solution.py:126
  43.4 1.9 %collective-permute-start.2 = (bf16[256,512]{1,0:T(8,128)(2,1)S(1)}, bf16[256,512]{1,0:T(8,128)(2,1)S(1)}, u32[]{:S(2)}, u32[]{:S(2)}) collective-permute-start(bf16[256,512]{1,0:T(8,128)(2,1)S(1)} %bitcast.8), channel_id=1, source_target_pairs={{0,2},{1,3},{2,4},{3,5},{4,6},{5,7},{6,8},{7,9},{8,10},{9,11},{10,... | collective-permute-start | bytes 786440 | tf_op jit(solution)/shard_map/ppermute | solution.py:126
  45.4 0.0 copy-done
  45.4 0.1 copy.10
  45.6 0.1 reshape.21
  45.7 0.1 reshape.22.doms
  45.8 0.7 reshape.23.owner
  46.5 0.9 %fusion = pred[16]{0:T(512)(128)(4,1)S(1)} fusion(s32[16,16]{1,0:T(8,128)} %param.8, s32[]{:T(128)S(6)} %select_n.29), kind=kLoop, calls=%fused_computation.3 | loop fusion | flops 16 | bytes 84 | tf_op jit(solution)/shard_map/gt | solution.py:134
  47.4 3.9 %collective-permute-done.1.refs_1_ = bf16[256,512]{1,0:T(8,128)(2,1)S(1)} collective-permute-done((bf16[256,512]{1,0:T(8,128)(2,1)S(1)}, bf16[256,512]{1,0:T(8,128)(2,1)S(1)}, u32[]{:S(2)}, u32[]{:S(2)}) %collective-permute-start.1) | collective-permute-done | bytes 262176 | tf_op jit(solution)/shard_map/ppermute | solution.py:130
  51.2 3.0 %collective-permute-start.4 = (bf16[256,512]{1,0:T(8,128)(2,1)S(1)}, bf16[256,512]{1,0:T(8,128)(2,1)S(1)}, u32[]{:S(2)}, u32[]{:S(2)}) collective-permute-start(bf16[256,512]{1,0:T(8,128)(2,1)S(1)} %collective-permute-done.1.refs_1_), channel_id=1, source_target_pairs={{0,2},{1,3},{2,4},{3,5},{4,6},{5,7},{6,8},{7,9},{8,10},{9,11},{10,... | collective-permute-start | bytes 786440 | tf_op jit(solution)/shard_map/ppermute | solution.py:126
  54.2 0.1 convert_reduce_fusion
  54.3 0.1 select_reduce_fusion
  54.5 0.1 concatenate.3.place
  54.5 0.0 collective-permute-done.refs_2_
  54.6 4.1 %collective-permute-start.3 = (bf16[256,512]{1,0:T(8,128)(2,1)S(1)}, bf16[256,512]{1,0:T(8,128)(2,1)S(1)}, u32[]{:S(2)}, u32[]{:S(2)}) collective-permute-start(bf16[256,512]{1,0:T(8,128)(2,1)S(1)} %collective-permute-done.refs_2_), channel_id=1, source_target_pairs={{0,30},{1,31},{2,0},{3,1},{4,2},{5,3},{6,4},{7,5},{8,6},{9,7},{10,... | collective-permute-start | bytes 786440 | tf_op jit(solution)/shard_map/ppermute | solution.py:126
  58.6 2.7 %collective-permute-start.5 = (bf16[256,512]{1,0:T(8,128)(2,1)S(1)}, bf16[256,512]{1,0:T(8,128)(2,1)S(1)}, u32[]{:S(2)}, u32[]{:S(2)}) collective-permute-start(bf16[256,512]{1,0:T(8,128)(2,1)S(1)} %collective-permute-done.1.refs_1_), channel_id=1, source_target_pairs={{0,30},{1,31},{2,0},{3,1},{4,2},{5,3},{6,4},{7,5},{8,6},{9,7},{10,... | collective-permute-start | bytes 786440 | tf_op jit(solution)/shard_map/ppermute | solution.py:126
  61.3 0.0 collective-permute-done.4.refs_0_
  61.3 3.1 %collective-permute-start.6 = (bf16[256,512]{1,0:T(8,128)(2,1)S(1)}, bf16[256,512]{1,0:T(8,128)(2,1)S(1)}, u32[]{:S(2)}, u32[]{:S(2)}) collective-permute-start(bf16[256,512]{1,0:T(8,128)(2,1)S(1)} %collective-permute-done.4.refs_0_), channel_id=1, source_target_pairs={{0,2},{1,3},{2,4},{3,5},{4,6},{5,7},{6,8},{7,9},{8,10},{9,11},{10,... | collective-permute-start | bytes 786440 | tf_op jit(solution)/shard_map/ppermute | solution.py:126
  64.5 0.0 collective-permute-done.2.refs_3_
  64.5 0.0 collective-permute-done.3.refs_4_
  64.5 0.0 all-gather.2.cloned.1.call-done.refs_5_
  64.5 3.3 %shard_map.55 = (f32[160,256]{1,0:T(8,128)S(1)}, bf16[8,512,256]{2,1,0:T(8,128)(2,1)S(1)}) custom-call(s32[12]{0:T(128)S(1)} %concatenate.3.place, s32[16,128]{1,0:T(8,128)S(1)} %reshape.22.doms, bf16[256,512]{1,0:T(8,128)(2,1)S(1)} %bitcast.9, bf16[256,512]{1,0:T(8,128)(2,1)S(1)} %collective-permute-done.1.refs_1_, ...), custom_call_target="tpu_custom_call" | custom-call | flops 536870912 | bytes 2097152 | tf_op jit(solution)/shard_map/pallas_call | solution.py:158
  67.8 0.0 collective-permute-done.5.refs_1_
  67.8 3.0 %collective-permute-done.6.refs_2_ = bf16[256,512]{1,0:T(8,128)(2,1)S(1)} collective-permute-done((bf16[256,512]{1,0:T(8,128)(2,1)S(1)}, bf16[256,512]{1,0:T(8,128)(2,1)S(1)}, u32[]{:S(2)}, u32[]{:S(2)}) %collective-permute-start.6) | collective-permute-done | bytes 262176 | tf_op jit(solution)/shard_map/ppermute | solution.py:126
  70.8 2.9 %shard_map.56 = f32[256,256]{1,0:T(8,128)} custom-call(s32[12]{0:T(128)S(1)} %concatenate.3.place, s32[16,128]{1,0:T(8,128)S(1)} %reshape.22.doms, s32[16,256]{1,0:T(8,128)S(1)} %reshape.23.owner, f32[160,256]{1,0:T(8,128)S(1)} %get-tuple-element.15.part, bf16[8,512,256]{2,1,0:T(8,128)(2,1)S(1)} %get-tuple-element.16.blocks, ...), custom_call_target="tpu_custom_call" | custom-call | flops 536870912 | bytes 2097152 | tf_op jit(solution)/shard_map/pallas_call | solution.py:174
  (2 shorter events, 0.0 us)
Async XLA Ops:
  6.5 38.8 %copy-start = (s32[4096,8]{0,1:T(8,128)S(1)}, s32[4096,8]{0,1:T(8,128)}, u32[]{:S(2)}) copy-start(s32[4096,8]{0,1:T(8,128)} %param.6) | copy-start | bytes 393220
  6.5 58.0 %all-gather.2.cloned.1.call-start = ((), (), s32[]{:S(2)}) async-start(), calls=%async_computation | async-start | bytes 4456448 | tf_op jit(solution)/shard_map/all_gather | solution.py:117
  34.4 16.9 %collective-permute-start.1 = (bf16[256,512]{1,0:T(8,128)(2,1)S(1)}, bf16[256,512]{1,0:T(8,128)(2,1)S(1)}, u32[]{:S(2)}, u32[]{:S(2)}) collective-permute-start(bf16[256,512]{1,0:T(8,128)(2,1)S(1)} %bitcast.6), channel_id=1, source_target_pairs={{0,1},{1,0},{2,3},{3,2},{4,5},{5,4},{6,7},{7,6},{8,9},{9,8},{10,11... | collective-permute-start | bytes 786440 | tf_op jit(solution)/shard_map/ppermute | solution.py:130
  39.5 15.1 %collective-permute-start = (bf16[256,512]{1,0:T(8,128)(2,1)S(1)}, bf16[256,512]{1,0:T(8,128)(2,1)S(1)}, u32[]{:S(2)}, u32[]{:S(2)}) collective-permute-start(bf16[256,512]{1,0:T(8,128)(2,1)S(1)} %bitcast.7), channel_id=1, source_target_pairs={{0,30},{1,31},{2,0},{3,1},{4,2},{5,3},{6,4},{7,5},{8,6},{9,7},{10,... | collective-permute-start | bytes 786440 | tf_op jit(solution)/shard_map/ppermute | solution.py:126
  43.4 21.1 %collective-permute-start.2 = (bf16[256,512]{1,0:T(8,128)(2,1)S(1)}, bf16[256,512]{1,0:T(8,128)(2,1)S(1)}, u32[]{:S(2)}, u32[]{:S(2)}) collective-permute-start(bf16[256,512]{1,0:T(8,128)(2,1)S(1)} %bitcast.8), channel_id=1, source_target_pairs={{0,2},{1,3},{2,4},{3,5},{4,6},{5,7},{6,8},{7,9},{8,10},{9,11},{10,... | collective-permute-start | bytes 786440 | tf_op jit(solution)/shard_map/ppermute | solution.py:126
  51.2 10.1 %collective-permute-start.4 = (bf16[256,512]{1,0:T(8,128)(2,1)S(1)}, bf16[256,512]{1,0:T(8,128)(2,1)S(1)}, u32[]{:S(2)}, u32[]{:S(2)}) collective-permute-start(bf16[256,512]{1,0:T(8,128)(2,1)S(1)} %collective-permute-done.1.refs_1_), channel_id=1, source_target_pairs={{0,2},{1,3},{2,4},{3,5},{4,6},{5,7},{6,8},{7,9},{8,10},{9,11},{10,... | collective-permute-start | bytes 786440 | tf_op jit(solution)/shard_map/ppermute | solution.py:126
  54.6 10.0 %collective-permute-start.3 = (bf16[256,512]{1,0:T(8,128)(2,1)S(1)}, bf16[256,512]{1,0:T(8,128)(2,1)S(1)}, u32[]{:S(2)}, u32[]{:S(2)}) collective-permute-start(bf16[256,512]{1,0:T(8,128)(2,1)S(1)} %collective-permute-done.refs_2_), channel_id=1, source_target_pairs={{0,30},{1,31},{2,0},{3,1},{4,2},{5,3},{6,4},{7,5},{8,6},{9,7},{10,... | collective-permute-start | bytes 786440 | tf_op jit(solution)/shard_map/ppermute | solution.py:126
  58.6 9.2 %collective-permute-start.5 = (bf16[256,512]{1,0:T(8,128)(2,1)S(1)}, bf16[256,512]{1,0:T(8,128)(2,1)S(1)}, u32[]{:S(2)}, u32[]{:S(2)}) collective-permute-start(bf16[256,512]{1,0:T(8,128)(2,1)S(1)} %collective-permute-done.1.refs_1_), channel_id=1, source_target_pairs={{0,30},{1,31},{2,0},{3,1},{4,2},{5,3},{6,4},{7,5},{8,6},{9,7},{10,... | collective-permute-start | bytes 786440 | tf_op jit(solution)/shard_map/ppermute | solution.py:126
  61.3 9.5 %collective-permute-start.6 = (bf16[256,512]{1,0:T(8,128)(2,1)S(1)}, bf16[256,512]{1,0:T(8,128)(2,1)S(1)}, u32[]{:S(2)}, u32[]{:S(2)}) collective-permute-start(bf16[256,512]{1,0:T(8,128)(2,1)S(1)} %collective-permute-done.4.refs_0_), channel_id=1, source_target_pairs={{0,2},{1,3},{2,4},{3,5},{4,6},{5,7},{6,8},{7,9},{8,10},{9,11},{10,... | collective-permute-start | bytes 786440 | tf_op jit(solution)/shard_map/ppermute | solution.py:126
Sparse Core Ops, SparseCore 0:
  9.5 52.0 all-gather.1

commit v3 on v2

v3 whole, which is shorter than its diff:
```python
import jax
import jax.numpy as jnp
from jax import lax
from jax.experimental import pallas as pl
from jax.experimental.pallas import tpu as pltpu
from jax.sharding import PartitionSpec as P


HALF_Y = 2
STRIDE = 4
HEAD = 4
HEAD_MIB = 48
MIB = 2**20


EARLY = ((0, 0), (0, 1), (1, 0), (3, 0), (2, 0), (3, 1), (1, 1))
LATE = ((2, 1),)


def picks_of(kinds, place, doms, n_act, k):
    residue, half = place[1], place[3]
    width = doms.shape[1]
    chunk = width // k
    lane = lax.broadcasted_iota(jnp.int32, (width, width), 1)
    other = lax.broadcasted_iota(jnp.int32, (width, width), 0)
    same = (lane // k == other // k).astype(jnp.float32).astype(jnp.bfloat16)
    table = doms[...]
    inside = (table == place[0]).astype(jnp.float32).astype(jnp.bfloat16)
    hits = jnp.dot(inside, same, preferred_element_type=jnp.float32)
    table = jnp.where(hits > 0, table, -2)
    table_row = lax.broadcasted_iota(jnp.int32, table.shape, 0)
    rows = n_act * chunk
    row = lax.broadcasted_iota(jnp.int32, (rows, width), 0)
    lane = lax.broadcasted_iota(jnp.int32, (rows, width), 1)
    wanted = jnp.full((rows, width), -1, jnp.int32)
    for i in range(n_act):
        wanted = jnp.where(row // chunk == i, place[HEAD + i], wanted)
    wanted = jnp.where(lane // k == row % chunk, wanted, -1)
    per = doms.shape[0] // (HALF_Y * STRIDE)
    picks = []
    for step, across in kinds:
        base = ((half ^ across) * STRIDE + lax.rem(residue + step, STRIDE)) * per
        for j in range(per):
            line = jnp.max(jnp.where(table_row == base + j, table, -2), axis=0, keepdims=True)
            picks.append((line == wanted).astype(jnp.float32).astype(jnp.bfloat16))
    return picks


def expand(picks, pieces, tiles):
    n_act, count, _ = tiles.shape
    chunk = count // len(picks)
    width = picks[0].shape[1]
    per = len(picks) // len(pieces)
    for n, pick in enumerate(picks):
        piece = pieces[n // per][pl.ds(n % per * width, width), :]
        got = jnp.dot(pick, piece, preferred_element_type=jnp.float32)
        for i in range(n_act):
            tiles[i, n * chunk : (n + 1) * chunk, :] = got[i * chunk : (i + 1) * chunk].astype(jnp.bfloat16)


def order_of(kinds, own, place, per_z):
    residue, half = place[1], place[3]
    share = STRIDE * per_z
    shape = (own.shape[0], len(kinds) * share)
    at = lax.broadcasted_iota(jnp.int32, (1, shape[1]), 1)
    slot = jnp.zeros((1, shape[1]), jnp.int32)
    for n, (step, across) in enumerate(kinds):
        inner = at - n * share
        z = inner // per_z * STRIDE + lax.rem(residue + step, STRIDE)
        slot = jnp.where(inner >= 0, (z * HALF_Y + (half ^ across)) * per_z + inner % per_z, slot)
    return (own[:, : shape[1]] == slot).astype(jnp.float32)


def reorder(order, rows):
    return jnp.dot(order, rows, precision=lax.Precision.HIGHEST, preferred_element_type=jnp.float32)


def head_kernel(place, doms, owner, *refs):
    pieces = refs[: len(EARLY)]
    integrals, part, blocks, late_picks, late_order, tiles, sem = refs[len(EARLY) :]
    n_act, depth, _ = blocks.shape

    def fetch(i):
        start = pl.multiple_of(place[HEAD + i] * depth, depth)
        return pltpu.make_async_copy(integrals.at[pl.ds(start, depth), :], blocks.at[i], sem.at[i])

    for i in range(n_act):
        fetch(i).start()
    pairs = part.shape[0]
    per_z = tiles.shape[1] // (len(EARLY) * STRIDE)
    k = doms.shape[0] * doms.shape[1] // pairs
    picks = picks_of(EARLY + LATE, place, doms, n_act, k)
    n_late = late_picks.shape[0]
    for n, pick in enumerate(picks[-n_late:]):
        late_picks[n] = pick
    expand(picks[:-n_late], pieces, tiles)
    own = owner[pl.ds(place[2], 1), :] - place[2] * pairs
    own = jnp.transpose(jnp.broadcast_to(own, (pairs, pairs)))
    late_order[...] = order_of(LATE, own, place, per_z)
    order = order_of(EARLY, own, place, per_z)
    total = jnp.zeros((tiles.shape[1], part.shape[1]), jnp.float32)
    for i in range(n_act):
        fetch(i).wait()
        total = total + jnp.dot(tiles[i], blocks[i], preferred_element_type=jnp.float32)
    part[...] = reorder(order, total)


def finish_kernel(part, blocks, late_picks, late_order, *refs):
    pieces, (out, tiles) = refs[: len(LATE)], refs[len(LATE) :]
    expand([late_picks[n] for n in range(late_picks.shape[0])], pieces, tiles)
    total = jnp.zeros((tiles.shape[1], out.shape[1]), jnp.float32)
    for i in range(tiles.shape[0]):
        total = total + jnp.dot(tiles[i], blocks[i], preferred_element_type=jnp.float32)
    out[...] = part[...] + reorder(late_order[...], total)


def on_device(amps, domains, owner, coupling, integrals):
    n_blk, n_grp = lax.axis_size("blk"), lax.axis_size("grp")
    n_z = n_grp // HALF_Y
    me_blk, me_grp = lax.axis_index("blk"), lax.axis_index("grp")
    me_z = me_grp // HALF_Y
    depth, cols = integrals.shape
    nvb = coupling.shape[0]
    n_act = nvb // 2
    slots, k, _ = amps.shape
    pairs = slots * n_grp

    whole = lax.all_gather(integrals, "blk", axis=0, tiled=True)

    strided = [
        [(i * STRIDE + q) * HALF_Y + y for i in range(n_z // STRIDE)]
        for q in range(STRIDE)
        for y in range(HALF_Y)
    ]

    def send(x, hops):
        return lax.ppermute(x, "grp", [(g, (g + hops * HALF_Y) % n_grp) for g in range(n_grp)])

    near = lax.all_gather(amps, "grp", axis=0, tiled=True, axis_index_groups=strided)
    near = near.reshape(near.shape[0] * k, depth)
    near_x = lax.ppermute(near, "grp", [(g, g ^ 1) for g in range(n_grp)])
    up = send(near, -1)
    down = send(near, 1)

    keep = lax.dynamic_index_in_dim(coupling, me_z, axis=1, keepdims=False) > 0
    numbers = jnp.arange(nvb, dtype=jnp.int32)
    before = jnp.sum((numbers[None, :] < numbers[:, None]) & keep[None, :], axis=1)
    chosen = keep[None, :] & (before[None, :] == jnp.arange(n_act)[:, None])
    act = jnp.sum(jnp.where(chosen, numbers[None, :], 0), axis=1)
    head = jnp.stack([me_z, me_z % STRIDE, me_blk, me_grp % HALF_Y])
    place = jnp.concatenate([head, act]).astype(jnp.int32)
    mine = lax.dynamic_slice_in_dim(domains, me_blk * pairs, pairs)
    mine = mine.reshape(n_z // STRIDE, STRIDE, HALF_Y, slots * k)
    doms = jnp.transpose(mine, (2, 1, 0, 3)).reshape(-1, 2 * slots * k)
    owners = owner.reshape(n_blk, pairs)
    ready, place, doms, owners = lax.optimization_barrier((up, place, doms, owners))
    far = send(ready, -1)
    down_x = send(near_x, 1)
    up_x = send(near_x, -1)
    far_x = lax.ppermute(far, "grp", [(g, g ^ 1) for g in range(n_grp)])
    vmem = pl.BlockSpec(memory_space=pltpu.VMEM)
    smem = pl.BlockSpec(memory_space=pltpu.SMEM)

    def cost(flops):
        return pl.CostEstimate(flops=flops, bytes_accessed=2 * MIB, transcendentals=0)

    early, late = (near, near_x, up, down, far, down_x, up_x), (far_x,)
    n_early, n_late = (sum(p.shape[0] for p in ps) // k for ps in (early, late))
    chunk = doms.shape[1] // k
    prepared = (
        jax.ShapeDtypeStruct((pairs, cols), jnp.float32),
        jax.ShapeDtypeStruct((n_act, depth, cols), jnp.bfloat16),
        jax.ShapeDtypeStruct((n_late // chunk, n_act * chunk, doms.shape[1]), jnp.bfloat16),
        jax.ShapeDtypeStruct((pairs, n_late), jnp.float32),
    )
    prepared = pl.pallas_call(
        head_kernel,
        in_specs=[smem] + [vmem] * (2 + len(early)) + [pl.BlockSpec(memory_space=pl.ANY)],
        out_specs=(vmem,) * len(prepared),
        out_shape=prepared,
        scratch_shapes=[
            pltpu.VMEM((n_act, n_early, depth), jnp.bfloat16),
            pltpu.SemaphoreType.DMA((n_act,)),
        ],
        compiler_params=pltpu.CompilerParams(vmem_limit_bytes=HEAD_MIB * MIB),
        cost_estimate=cost(2**29),
    )(place, doms, owners, *early, whole)
    return pl.pallas_call(
        finish_kernel,
        in_specs=[vmem] * (len(prepared) + len(late)),
        out_specs=vmem,
        out_shape=jax.ShapeDtypeStruct((pairs, cols), jnp.float32),
        scratch_shapes=[pltpu.VMEM((n_act, n_late, depth), jnp.bfloat16)],
        compiler_params=pltpu.CompilerParams(vmem_limit_bytes=16 * MIB),
        cost_estimate=cost(2**27),
    )(*prepared, *late)


def solution(mesh):
    return jax.shard_map(
        on_device,
        mesh=mesh,
        in_specs=(P(("blk", "grp"), None, None), P(), P(), P(), P("blk", "grp")),
        out_specs=P("blk", "grp"),
        check_vma=False,
    )
```

time: 81 us -> 83.1 us (1.026)
  starting transfers between devices: 23.9 us -> 25.4 us
    ppermute x6 -> x5, waiting for transfers between devices: 3.02 us -> 7.23 us  [send(): lax.ppermute(x, 'grp', [(g, (g + hops * HALF_Y) % n_grp) for g in range(n...]
    ppermute x1, waiting for transfers between devices: 3.86 us -> 0.01 us  [on_device(): near_x = lax.ppermute(near, 'grp', [(g, g ^ 1) for g in range(n_grp)])]
    ppermute x0 -> x1, starting transfers between devices: none -> 2.24 us  [on_device(): far_x = lax.ppermute(far, 'grp', [(g, g ^ 1) for g in range(n_grp)])]
    ppermute x6 -> x5, starting transfers between devices: 18.8 us -> 18.1 us  [send(): lax.ppermute(x, 'grp', [(g, (g + hops * HALF_Y) % n_grp) for g in range(n...]
  transfers between devices with their start and end apart: 8 -> 8, of which waited for: 2 -> 2; matrix products, arithmetic and copies ran while one was open for 3% -> 3% of each run, Pallas kernels for 4% -> 5%
where the time goes in v3:
time: 83.1 us; the launch traced here: 82.6 us
  blocking collectives  27.1 us (33%)
  starting transfers between devices  25.4 us (31%)
  between operations  13.6 us (16%)
  waiting for transfers between devices  7.95 us (10%)
  Pallas kernels  6.32 us (8%)
  local copies, waits for them, and re-layouts  1.14 us (1%)
  other arithmetic  1.12 us (1%)
    all_gather x1, blocking collectives, on_device(): lax.all_gather(amps, 'grp', axis=0, tiled=True, axis_index_groups=strided)  27.1 us
    ppermute x5, starting transfers between devices, send(): lax.ppermute(x, 'grp', [(g, (g + hops * HALF_Y) % n_grp) for g in range(n...  18.1 us
    ppermute x5, waiting for transfers between devices, send(): lax.ppermute(x, 'grp', [(g, (g + hops * HALF_Y) % n_grp) for g in range(n...  7.23 us
    ppermute x1, starting transfers between devices, on_device(): near_x = lax.ppermute(near, 'grp', [(g, g ^ 1) for g in range(n_grp)])  5.09 us
    pallas_call x1, Pallas kernels, on_device(): pl.pallas_call(head_kernel, in_specs=[smem] + [vmem] * (2 + len(early)) +...  4.3 us
    ppermute x1, starting transfers between devices, on_device(): far_x = lax.ppermute(far, 'grp', [(g, g ^ 1) for g in range(n_grp)])  2.24 us
    pallas_call x1, Pallas kernels, on_device(): pl.pallas_call(finish_kernel, in_specs=[vmem] * (len(prepared) + len(late...  2.02 us
  transfers between devices with their start and end apart: 8, of which 2 were waited for; matrix products, arithmetic and copies ran while one was open for 3% of the time, Pallas kernels for 5%

profile of v3, /device:TPU:6, one launch (start us, length us, event | category | flops | bytes accessed | tf_op | source)
XLA Modules:
  0.0 82.6 jit_solution(9206223549247221479)
XLA Ops:
  6.5 0.0 copy-start
  6.5 0.0 all-gather.2.cloned.1.call-start
  6.5 0.7 all-gather.2.cloned.1.call-update
  7.3 27.1 %all_gather.6 = bf16[32,8,512]{2,1,0:T(8,128)(2,1)S(1)} all-gather(bf16[8,8,512]{2,1,0:T(8,128)(2,1)} %param.5), channel_id=1, replica_groups={{0,8,16,24},{1,9,17,25},{2,10,18,26},{3,11,19,27},{4,12,20,28},{5,13,21..., dimensions={0}, use_global_device_ids=true | all-gather | bytes 327680 | tf_op jit(solution)/shard_map/all_gather | solution.py:139
  34.4 5.1 %collective-permute-start.1 = (bf16[256,512]{1,0:T(8,128)(2,1)S(1)}, bf16[256,512]{1,0:T(8,128)(2,1)S(1)}, u32[]{:S(2)}, u32[]{:S(2)}) collective-permute-start(bf16[256,512]{1,0:T(8,128)(2,1)S(1)} %bitcast.6), channel_id=1, source_target_pairs={{0,1},{1,0},{2,3},{3,2},{4,5},{5,4},{6,7},{7,6},{8,9},{9,8},{10,11... | collective-permute-start | bytes 786440 | tf_op jit(solution)/shard_map/ppermute | solution.py:141
  39.5 4.0 %collective-permute-start = (bf16[256,512]{1,0:T(8,128)(2,1)S(1)}, bf16[256,512]{1,0:T(8,128)(2,1)S(1)}, u32[]{:S(2)}, u32[]{:S(2)}) collective-permute-start(bf16[256,512]{1,0:T(8,128)(2,1)S(1)} %bitcast.7), channel_id=1, source_target_pairs={{0,30},{1,31},{2,0},{3,1},{4,2},{5,3},{6,4},{7,5},{8,6},{9,7},{10,... | collective-permute-start | bytes 786440 | tf_op jit(solution)/shard_map/ppermute | solution.py:137
  43.5 0.9 %fusion = pred[16]{0:T(512)(128)(4,1)S(1)} fusion(s32[16,16]{1,0:T(8,128)} %param.8, s32[]{:T(128)S(6)} %select_n.29), kind=kLoop, calls=%fused_computation.3 | loop fusion | flops 16 | bytes 84 | tf_op jit(solution)/shard_map/gt | solution.py:145
  44.4 0.1 convert_reduce_fusion
  44.5 0.0 copy-done
  44.5 0.1 select_reduce_fusion
  44.6 0.7 reshape.23.owner
  45.4 0.1 copy.10
  45.5 0.1 reshape.21
  45.6 0.1 reshape.22.doms
  45.7 0.1 concatenate.3.place
  45.8 2.0 %collective-permute-done.refs_2_ = bf16[256,512]{1,0:T(8,128)(2,1)S(1)} collective-permute-done((bf16[256,512]{1,0:T(8,128)(2,1)S(1)}, bf16[256,512]{1,0:T(8,128)(2,1)S(1)}, u32[]{:S(2)}, u32[]{:S(2)}) %collective-permute-start) | collective-permute-done | bytes 262176 | tf_op jit(solution)/shard_map/ppermute | solution.py:137
  47.7 5.2 %collective-permute-start.3 = (bf16[256,512]{1,0:T(8,128)(2,1)S(1)}, bf16[256,512]{1,0:T(8,128)(2,1)S(1)}, u32[]{:S(2)}, u32[]{:S(2)}) collective-permute-start(bf16[256,512]{1,0:T(8,128)(2,1)S(1)} %collective-permute-done.refs_2_), channel_id=1, source_target_pairs={{0,30},{1,31},{2,0},{3,1},{4,2},{5,3},{6,4},{7,5},{8,6},{9,7},{10,... | collective-permute-start | bytes 786440 | tf_op jit(solution)/shard_map/ppermute | solution.py:137
  52.9 1.9 %collective-permute-start.2 = (bf16[256,512]{1,0:T(8,128)(2,1)S(1)}, bf16[256,512]{1,0:T(8,128)(2,1)S(1)}, u32[]{:S(2)}, u32[]{:S(2)}) collective-permute-start(bf16[256,512]{1,0:T(8,128)(2,1)S(1)} %bitcast.8), channel_id=1, source_target_pairs={{0,2},{1,3},{2,4},{3,5},{4,6},{5,7},{6,8},{7,9},{8,10},{9,11},{10,... | collective-permute-start | bytes 786440 | tf_op jit(solution)/shard_map/ppermute | solution.py:137
  54.8 0.0 collective-permute-done.1.refs_1_
  54.8 5.1 %collective-permute-start.5 = (bf16[256,512]{1,0:T(8,128)(2,1)S(1)}, bf16[256,512]{1,0:T(8,128)(2,1)S(1)}, u32[]{:S(2)}, u32[]{:S(2)}) collective-permute-start(bf16[256,512]{1,0:T(8,128)(2,1)S(1)} %collective-permute-done.1.refs_1_), channel_id=1, source_target_pairs={{0,30},{1,31},{2,0},{3,1},{4,2},{5,3},{6,4},{7,5},{8,6},{9,7},{10,... | collective-permute-start | bytes 786440 | tf_op jit(solution)/shard_map/ppermute | solution.py:137
  60.0 1.9 %collective-permute-start.4 = (bf16[256,512]{1,0:T(8,128)(2,1)S(1)}, bf16[256,512]{1,0:T(8,128)(2,1)S(1)}, u32[]{:S(2)}, u32[]{:S(2)}) collective-permute-start(bf16[256,512]{1,0:T(8,128)(2,1)S(1)} %collective-permute-done.1.refs_1_), channel_id=1, source_target_pairs={{0,2},{1,3},{2,4},{3,5},{4,6},{5,7},{6,8},{7,9},{8,10},{9,11},{10,... | collective-permute-start | bytes 786440 | tf_op jit(solution)/shard_map/ppermute | solution.py:137
  61.9 0.0 collective-permute-done.3.refs_4_
  61.9 2.2 %collective-permute-start.6 = (bf16[256,512]{1,0:T(8,128)(2,1)S(1)}, bf16[256,512]{1,0:T(8,128)(2,1)S(1)}, u32[]{:S(2)}, u32[]{:S(2)}) collective-permute-start(bf16[256,512]{1,0:T(8,128)(2,1)S(1)} %collective-permute-done.3.refs_4_), channel_id=1, source_target_pairs={{0,1},{1,0},{2,3},{3,2},{4,5},{5,4},{6,7},{7,6},{8,9},{9,8},{10,11... | collective-permute-start | bytes 786440 | tf_op jit(solution)/shard_map/ppermute | solution.py:160
  64.2 0.0 collective-permute-done.2.refs_3_
  64.2 0.0 collective-permute-done.5.refs_6_
  64.2 5.3 %collective-permute-done.4.refs_5_ = bf16[256,512]{1,0:T(8,128)(2,1)S(1)} collective-permute-done((bf16[256,512]{1,0:T(8,128)(2,1)S(1)}, bf16[256,512]{1,0:T(8,128)(2,1)S(1)}, u32[]{:S(2)}, u32[]{:S(2)}) %collective-permute-start.4) | collective-permute-done | bytes 262176 | tf_op jit(solution)/shard_map/ppermute | solution.py:137
  69.5 0.0 all-gather.2.cloned.1.call-done.refs_7_
  69.5 4.3 %shard_map.55 = (f32[256,256]{1,0:T(8,128)S(1)}, bf16[8,512,256]{2,1,0:T(8,128)(2,1)S(1)}, bf16[2,128,128]{2,1,0:T(8,128)(2,1)S(1)}, f32[256,32]{1,0:T(8,128)S(1)}) custom-call(s32[12]{0:T(128)S(1)} %concatenate.3.place, s32[16,128]{1,0:T(8,128)S(1)} %reshape.22.doms, s32[16,256]{1,0:T(8,128)S(1)} %reshape.23.owner, bf16[256,512]{1,0:T(8,128)(2,1)S(1)} %bitcast.9, ...), custom_call_target="tpu_custom_call" | custom-call | flops 536870912 | bytes 2097152 | tf_op jit(solution)/shard_map/pallas_call | solution.py:176
  73.8 0.0 collective-permute-done.6.refs_0_
  73.8 2.0 %shard_map.56 = f32[256,256]{1,0:T(8,128)} custom-call(f32[256,256]{1,0:T(8,128)S(1)} %get-tuple-element.17.part, bf16[8,512,256]{2,1,0:T(8,128)(2,1)S(1)} %get-tuple-element.18.blocks, bf16[2,128,128]{2,1,0:T(8,128)(2,1)S(1)} %get-tuple-element.19.late_picks, f32[256,32]{1,0:T(8,128)S(1)} %get-tuple-element.20.late_order, ...), custom_call_target="tpu_custom_call" | custom-call | flops 134217728 | bytes 2097152 | tf_op jit(solution)/shard_map/pallas_call | solution.py:188
  (2 shorter events, 0.0 us)
Async XLA Ops:
  6.5 37.9 %copy-start = (s32[4096,8]{0,1:T(8,128)S(1)}, s32[4096,8]{0,1:T(8,128)}, u32[]{:S(2)}) copy-start(s32[4096,8]{0,1:T(8,128)} %param.6) | copy-start | bytes 393220
  6.5 62.9 %all-gather.2.cloned.1.call-start = ((), (), s32[]{:S(2)}) async-start(), calls=%async_computation | async-start | bytes 4456448 | tf_op jit(solution)/shard_map/all_gather | solution.py:128
  34.4 20.5 %collective-permute-start.1 = (bf16[256,512]{1,0:T(8,128)(2,1)S(1)}, bf16[256,512]{1,0:T(8,128)(2,1)S(1)}, u32[]{:S(2)}, u32[]{:S(2)}) collective-permute-start(bf16[256,512]{1,0:T(8,128)(2,1)S(1)} %bitcast.6), channel_id=1, source_target_pairs={{0,1},{1,0},{2,3},{3,2},{4,5},{5,4},{6,7},{7,6},{8,9},{9,8},{10,11... | collective-permute-start | bytes 786440 | tf_op jit(solution)/shard_map/ppermute | solution.py:141
  39.5 8.3 %collective-permute-start = (bf16[256,512]{1,0:T(8,128)(2,1)S(1)}, bf16[256,512]{1,0:T(8,128)(2,1)S(1)}, u32[]{:S(2)}, u32[]{:S(2)}) collective-permute-start(bf16[256,512]{1,0:T(8,128)(2,1)S(1)} %bitcast.7), channel_id=1, source_target_pairs={{0,30},{1,31},{2,0},{3,1},{4,2},{5,3},{6,4},{7,5},{8,6},{9,7},{10,... | collective-permute-start | bytes 786440 | tf_op jit(solution)/shard_map/ppermute | solution.py:137
  47.7 14.2 %collective-permute-start.3 = (bf16[256,512]{1,0:T(8,128)(2,1)S(1)}, bf16[256,512]{1,0:T(8,128)(2,1)S(1)}, u32[]{:S(2)}, u32[]{:S(2)}) collective-permute-start(bf16[256,512]{1,0:T(8,128)(2,1)S(1)} %collective-permute-done.refs_2_), channel_id=1, source_target_pairs={{0,30},{1,31},{2,0},{3,1},{4,2},{5,3},{6,4},{7,5},{8,6},{9,7},{10,... | collective-permute-start | bytes 786440 | tf_op jit(solution)/shard_map/ppermute | solution.py:137
  52.9 11.3 %collective-permute-start.2 = (bf16[256,512]{1,0:T(8,128)(2,1)S(1)}, bf16[256,512]{1,0:T(8,128)(2,1)S(1)}, u32[]{:S(2)}, u32[]{:S(2)}) collective-permute-start(bf16[256,512]{1,0:T(8,128)(2,1)S(1)} %bitcast.8), channel_id=1, source_target_pairs={{0,2},{1,3},{2,4},{3,5},{4,6},{5,7},{6,8},{7,9},{8,10},{9,11},{10,... | collective-permute-start | bytes 786440 | tf_op jit(solution)/shard_map/ppermute | solution.py:137
  54.8 9.3 %collective-permute-start.5 = (bf16[256,512]{1,0:T(8,128)(2,1)S(1)}, bf16[256,512]{1,0:T(8,128)(2,1)S(1)}, u32[]{:S(2)}, u32[]{:S(2)}) collective-permute-start(bf16[256,512]{1,0:T(8,128)(2,1)S(1)} %collective-permute-done.1.refs_1_), channel_id=1, source_target_pairs={{0,30},{1,31},{2,0},{3,1},{4,2},{5,3},{6,4},{7,5},{8,6},{9,7},{10,... | collective-permute-start | bytes 786440 | tf_op jit(solution)/shard_map/ppermute | solution.py:137
  60.0 9.5 %collective-permute-start.4 = (bf16[256,512]{1,0:T(8,128)(2,1)S(1)}, bf16[256,512]{1,0:T(8,128)(2,1)S(1)}, u32[]{:S(2)}, u32[]{:S(2)}) collective-permute-start(bf16[256,512]{1,0:T(8,128)(2,1)S(1)} %collective-permute-done.1.refs_1_), channel_id=1, source_target_pairs={{0,2},{1,3},{2,4},{3,5},{4,6},{5,7},{6,8},{7,9},{8,10},{9,11},{10,... | collective-permute-start | bytes 786440 | tf_op jit(solution)/shard_map/ppermute | solution.py:137
  61.9 11.8 %collective-permute-start.6 = (bf16[256,512]{1,0:T(8,128)(2,1)S(1)}, bf16[256,512]{1,0:T(8,128)(2,1)S(1)}, u32[]{:S(2)}, u32[]{:S(2)}) collective-permute-start(bf16[256,512]{1,0:T(8,128)(2,1)S(1)} %collective-permute-done.3.refs_4_), channel_id=1, source_target_pairs={{0,1},{1,0},{2,3},{3,2},{4,5},{5,4},{6,7},{7,6},{8,9},{9,8},{10,11... | collective-permute-start | bytes 786440 | tf_op jit(solution)/shard_map/ppermute | solution.py:160
Sparse Core Ops, SparseCore 0:
  9.5 52.0 all-gather.1

commit v4 on v3

--- a/solution.py
+++ b/solution.py
@@ -68,11 +68,20 @@
         inner = at - n * share
         z = inner // per_z * STRIDE + lax.rem(residue + step, STRIDE)
         slot = jnp.where(inner >= 0, (z * HALF_Y + (half ^ across)) * per_z + inner % per_z, slot)
-    return (own[:, : shape[1]] == slot).astype(jnp.float32)
+    return (own[:, : shape[1]] == slot).astype(jnp.float32).astype(jnp.bfloat16)
 
 
 def reorder(order, rows):
-    return jnp.dot(order, rows, precision=lax.Precision.HIGHEST, preferred_element_type=jnp.float32)
+    parts = []
+    for _ in range(3):
+        part = rows.astype(jnp.bfloat16)
+        rows = rows - part.astype(jnp.float32)
+        parts.append(part)
+    return jnp.dot(
+        jnp.concatenate([order] * 3, axis=1),
+        jnp.concatenate(parts, axis=0),
+        preferred_element_type=jnp.float32,
+    )
 
 
 def head_kernel(place, doms, owner, *refs):
@@ -171,7 +180,7 @@
         jax.ShapeDtypeStruct((pairs, cols), jnp.float32),
         jax.ShapeDtypeStruct((n_act, depth, cols), jnp.bfloat16),
         jax.ShapeDtypeStruct((n_late // chunk, n_act * chunk, doms.shape[1]), jnp.bfloat16),
-        jax.ShapeDtypeStruct((pairs, n_late), jnp.float32),
+        jax.ShapeDtypeStruct((pairs, n_late), jnp.bfloat16),
     )
     prepared = pl.pallas_call(
         head_kernel,

time: 83.1 us -> 82.4 us (level)
  no operation moved by 1% of the time
where the time goes in v4:
time: 82.4 us; the launch traced here: 81.9 us
  blocking collectives  27.1 us (33%)
  starting transfers between devices  25.4 us (31%)
  between operations  13.6 us (17%)
  waiting for transfers between devices  7.95 us (10%)
  Pallas kernels  5.58 us (7%)
  local copies, waits for them, and re-layouts  1.14 us (1%)
  other arithmetic  1.12 us (1%)
    all_gather x1, blocking collectives, on_device(): lax.all_gather(amps, 'grp', axis=0, tiled=True, axis_index_groups=strided)  27.1 us
    ppermute x5, starting transfers between devices, send(): lax.ppermute(x, 'grp', [(g, (g + hops * HALF_Y) % n_grp) for g in range(n...  18.1 us
    ppermute x5, waiting for transfers between devices, send(): lax.ppermute(x, 'grp', [(g, (g + hops * HALF_Y) % n_grp) for g in range(n...  7.23 us
    ppermute x1, starting transfers between devices, on_device(): near_x = lax.ppermute(near, 'grp', [(g, g ^ 1) for g in range(n_grp)])  5.09 us
    pallas_call x1, Pallas kernels, on_device(): pl.pallas_call(head_kernel, in_specs=[smem] + [vmem] * (2 + len(early)) +...  4.07 us
    ppermute x1, starting transfers between devices, on_device(): far_x = lax.ppermute(far, 'grp', [(g, g ^ 1) for g in range(n_grp)])  2.24 us
  transfers between devices with their start and end apart: 8, of which 2 were waited for; matrix products, arithmetic and copies ran while one was open for 3% of the time, Pallas kernels for 5%

profile of v4, /device:TPU:6, one launch (start us, length us, event | category | flops | bytes accessed | tf_op | source)
XLA Modules:
  0.0 81.9 jit_solution(16913005362771182954)
XLA Ops:
  6.5 0.0 copy-start
  6.5 0.0 all-gather.2.cloned.1.call-start
  6.5 0.7 all-gather.2.cloned.1.call-update
  7.3 27.1 %all_gather.6 = bf16[32,8,512]{2,1,0:T(8,128)(2,1)S(1)} all-gather(bf16[8,8,512]{2,1,0:T(8,128)(2,1)} %param.5), channel_id=1, replica_groups={{0,8,16,24},{1,9,17,25},{2,10,18,26},{3,11,19,27},{4,12,20,28},{5,13,21..., dimensions={0}, use_global_device_ids=true | all-gather | bytes 327680 | tf_op jit(solution)/shard_map/all_gather | solution.py:148
  34.4 5.1 %collective-permute-start.1 = (bf16[256,512]{1,0:T(8,128)(2,1)S(1)}, bf16[256,512]{1,0:T(8,128)(2,1)S(1)}, u32[]{:S(2)}, u32[]{:S(2)}) collective-permute-start(bf16[256,512]{1,0:T(8,128)(2,1)S(1)} %bitcast.6), channel_id=1, source_target_pairs={{0,1},{1,0},{2,3},{3,2},{4,5},{5,4},{6,7},{7,6},{8,9},{9,8},{10,11... | collective-permute-start | bytes 786440 | tf_op jit(solution)/shard_map/ppermute | solution.py:150
  39.5 4.0 %collective-permute-start = (bf16[256,512]{1,0:T(8,128)(2,1)S(1)}, bf16[256,512]{1,0:T(8,128)(2,1)S(1)}, u32[]{:S(2)}, u32[]{:S(2)}) collective-permute-start(bf16[256,512]{1,0:T(8,128)(2,1)S(1)} %bitcast.7), channel_id=1, source_target_pairs={{0,30},{1,31},{2,0},{3,1},{4,2},{5,3},{6,4},{7,5},{8,6},{9,7},{10,... | collective-permute-start | bytes 786440 | tf_op jit(solution)/shard_map/ppermute | solution.py:146
  43.5 0.9 %fusion = pred[16]{0:T(512)(128)(4,1)S(1)} fusion(s32[16,16]{1,0:T(8,128)} %param.8, s32[]{:T(128)S(6)} %select_n.29), kind=kLoop, calls=%fused_computation.3 | loop fusion | flops 16 | bytes 84 | tf_op jit(solution)/shard_map/gt | solution.py:154
  44.4 0.1 convert_reduce_fusion
  44.5 0.0 copy-done
  44.5 0.1 select_reduce_fusion
  44.6 0.7 reshape.23.owner
  45.4 0.1 copy.10
  45.5 0.1 reshape.21
  45.6 0.1 reshape.22.doms
  45.7 0.1 concatenate.3.place
  45.8 2.0 %collective-permute-done.refs_2_ = bf16[256,512]{1,0:T(8,128)(2,1)S(1)} collective-permute-done((bf16[256,512]{1,0:T(8,128)(2,1)S(1)}, bf16[256,512]{1,0:T(8,128)(2,1)S(1)}, u32[]{:S(2)}, u32[]{:S(2)}) %collective-permute-start) | collective-permute-done | bytes 262176 | tf_op jit(solution)/shard_map/ppermute | solution.py:146
  47.7 5.2 %collective-permute-start.3 = (bf16[256,512]{1,0:T(8,128)(2,1)S(1)}, bf16[256,512]{1,0:T(8,128)(2,1)S(1)}, u32[]{:S(2)}, u32[]{:S(2)}) collective-permute-start(bf16[256,512]{1,0:T(8,128)(2,1)S(1)} %collective-permute-done.refs_2_), channel_id=1, source_target_pairs={{0,30},{1,31},{2,0},{3,1},{4,2},{5,3},{6,4},{7,5},{8,6},{9,7},{10,... | collective-permute-start | bytes 786440 | tf_op jit(solution)/shard_map/ppermute | solution.py:146
  52.9 1.9 %collective-permute-start.2 = (bf16[256,512]{1,0:T(8,128)(2,1)S(1)}, bf16[256,512]{1,0:T(8,128)(2,1)S(1)}, u32[]{:S(2)}, u32[]{:S(2)}) collective-permute-start(bf16[256,512]{1,0:T(8,128)(2,1)S(1)} %bitcast.8), channel_id=1, source_target_pairs={{0,2},{1,3},{2,4},{3,5},{4,6},{5,7},{6,8},{7,9},{8,10},{9,11},{10,... | collective-permute-start | bytes 786440 | tf_op jit(solution)/shard_map/ppermute | solution.py:146
  54.8 0.0 collective-permute-done.1.refs_1_
  54.8 5.1 %collective-permute-start.5 = (bf16[256,512]{1,0:T(8,128)(2,1)S(1)}, bf16[256,512]{1,0:T(8,128)(2,1)S(1)}, u32[]{:S(2)}, u32[]{:S(2)}) collective-permute-start(bf16[256,512]{1,0:T(8,128)(2,1)S(1)} %collective-permute-done.1.refs_1_), channel_id=1, source_target_pairs={{0,30},{1,31},{2,0},{3,1},{4,2},{5,3},{6,4},{7,5},{8,6},{9,7},{10,... | collective-permute-start | bytes 786440 | tf_op jit(solution)/shard_map/ppermute | solution.py:146
  60.0 1.9 %collective-permute-start.4 = (bf16[256,512]{1,0:T(8,128)(2,1)S(1)}, bf16[256,512]{1,0:T(8,128)(2,1)S(1)}, u32[]{:S(2)}, u32[]{:S(2)}) collective-permute-start(bf16[256,512]{1,0:T(8,128)(2,1)S(1)} %collective-permute-done.1.refs_1_), channel_id=1, source_target_pairs={{0,2},{1,3},{2,4},{3,5},{4,6},{5,7},{6,8},{7,9},{8,10},{9,11},{10,... | collective-permute-start | bytes 786440 | tf_op jit(solution)/shard_map/ppermute | solution.py:146
  61.9 0.0 collective-permute-done.3.refs_4_
  61.9 2.2 %collective-permute-start.6 = (bf16[256,512]{1,0:T(8,128)(2,1)S(1)}, bf16[256,512]{1,0:T(8,128)(2,1)S(1)}, u32[]{:S(2)}, u32[]{:S(2)}) collective-permute-start(bf16[256,512]{1,0:T(8,128)(2,1)S(1)} %collective-permute-done.3.refs_4_), channel_id=1, source_target_pairs={{0,1},{1,0},{2,3},{3,2},{4,5},{5,4},{6,7},{7,6},{8,9},{9,8},{10,11... | collective-permute-start | bytes 786440 | tf_op jit(solution)/shard_map/ppermute | solution.py:169
  64.2 0.0 collective-permute-done.2.refs_3_
  64.2 0.0 collective-permute-done.5.refs_6_
  64.2 5.3 %collective-permute-done.4.refs_5_ = bf16[256,512]{1,0:T(8,128)(2,1)S(1)} collective-permute-done((bf16[256,512]{1,0:T(8,128)(2,1)S(1)}, bf16[256,512]{1,0:T(8,128)(2,1)S(1)}, u32[]{:S(2)}, u32[]{:S(2)}) %collective-permute-start.4) | collective-permute-done | bytes 262176 | tf_op jit(solution)/shard_map/ppermute | solution.py:146
  69.5 0.0 all-gather.2.cloned.1.call-done.refs_7_
  69.5 4.1 %shard_map.55 = (f32[256,256]{1,0:T(8,128)S(1)}, bf16[8,512,256]{2,1,0:T(8,128)(2,1)S(1)}, bf16[2,128,128]{2,1,0:T(8,128)(2,1)S(1)}, bf16[256,32]{1,0:T(8,128)(2,1)S(1)}) custom-call(s32[12]{0:T(128)S(1)} %concatenate.3.place, s32[16,128]{1,0:T(8,128)S(1)} %reshape.22.doms, s32[16,256]{1,0:T(8,128)S(1)} %reshape.23.owner, bf16[256,512]{1,0:T(8,128)(2,1)S(1)} %bitcast.9, ...), custom_call_target="tpu_custom_call" | custom-call | flops 536870912 | bytes 2097152 | tf_op jit(solution)/shard_map/pallas_call | solution.py:185
  73.5 0.0 collective-permute-done.6.refs_0_
  73.6 1.5 %shard_map.56 = f32[256,256]{1,0:T(8,128)} custom-call(f32[256,256]{1,0:T(8,128)S(1)} %get-tuple-element.17.part, bf16[8,512,256]{2,1,0:T(8,128)(2,1)S(1)} %get-tuple-element.18.blocks, bf16[2,128,128]{2,1,0:T(8,128)(2,1)S(1)} %get-tuple-element.19.late_picks, bf16[256,32]{1,0:T(8,128)(2,1)S(1)} %get-tuple-element.20.late_order, ...), custom_call_target="tpu_custom_call" | custom-call | flops 134217728 | bytes 2097152 | tf_op jit(solution)/shard_map/pallas_call | solution.py:197
  (2 shorter events, 0.0 us)
Async XLA Ops:
  6.5 37.9 %copy-start = (s32[4096,8]{0,1:T(8,128)S(1)}, s32[4096,8]{0,1:T(8,128)}, u32[]{:S(2)}) copy-start(s32[4096,8]{0,1:T(8,128)} %param.6) | copy-start | bytes 393220
  6.5 62.9 %all-gather.2.cloned.1.call-start = ((), (), s32[]{:S(2)}) async-start(), calls=%async_computation | async-start | bytes 4456448 | tf_op jit(solution)/shard_map/all_gather | solution.py:137
  34.4 20.5 %collective-permute-start.1 = (bf16[256,512]{1,0:T(8,128)(2,1)S(1)}, bf16[256,512]{1,0:T(8,128)(2,1)S(1)}, u32[]{:S(2)}, u32[]{:S(2)}) collective-permute-start(bf16[256,512]{1,0:T(8,128)(2,1)S(1)} %bitcast.6), channel_id=1, source_target_pairs={{0,1},{1,0},{2,3},{3,2},{4,5},{5,4},{6,7},{7,6},{8,9},{9,8},{10,11... | collective-permute-start | bytes 786440 | tf_op jit(solution)/shard_map/ppermute | solution.py:150
  39.5 8.3 %collective-permute-start = (bf16[256,512]{1,0:T(8,128)(2,1)S(1)}, bf16[256,512]{1,0:T(8,128)(2,1)S(1)}, u32[]{:S(2)}, u32[]{:S(2)}) collective-permute-start(bf16[256,512]{1,0:T(8,128)(2,1)S(1)} %bitcast.7), channel_id=1, source_target_pairs={{0,30},{1,31},{2,0},{3,1},{4,2},{5,3},{6,4},{7,5},{8,6},{9,7},{10,... | collective-permute-start | bytes 786440 | tf_op jit(solution)/shard_map/ppermute | solution.py:146
  47.7 14.2 %collective-permute-start.3 = (bf16[256,512]{1,0:T(8,128)(2,1)S(1)}, bf16[256,512]{1,0:T(8,128)(2,1)S(1)}, u32[]{:S(2)}, u32[]{:S(2)}) collective-permute-start(bf16[256,512]{1,0:T(8,128)(2,1)S(1)} %collective-permute-done.refs_2_), channel_id=1, source_target_pairs={{0,30},{1,31},{2,0},{3,1},{4,2},{5,3},{6,4},{7,5},{8,6},{9,7},{10,... | collective-permute-start | bytes 786440 | tf_op jit(solution)/shard_map/ppermute | solution.py:146
  52.9 11.3 %collective-permute-start.2 = (bf16[256,512]{1,0:T(8,128)(2,1)S(1)}, bf16[256,512]{1,0:T(8,128)(2,1)S(1)}, u32[]{:S(2)}, u32[]{:S(2)}) collective-permute-start(bf16[256,512]{1,0:T(8,128)(2,1)S(1)} %bitcast.8), channel_id=1, source_target_pairs={{0,2},{1,3},{2,4},{3,5},{4,6},{5,7},{6,8},{7,9},{8,10},{9,11},{10,... | collective-permute-start | bytes 786440 | tf_op jit(solution)/shard_map/ppermute | solution.py:146
  54.8 9.3 %collective-permute-start.5 = (bf16[256,512]{1,0:T(8,128)(2,1)S(1)}, bf16[256,512]{1,0:T(8,128)(2,1)S(1)}, u32[]{:S(2)}, u32[]{:S(2)}) collective-permute-start(bf16[256,512]{1,0:T(8,128)(2,1)S(1)} %collective-permute-done.1.refs_1_), channel_id=1, source_target_pairs={{0,30},{1,31},{2,0},{3,1},{4,2},{5,3},{6,4},{7,5},{8,6},{9,7},{10,... | collective-permute-start | bytes 786440 | tf_op jit(solution)/shard_map/ppermute | solution.py:146
  60.0 9.5 %collective-permute-start.4 = (bf16[256,512]{1,0:T(8,128)(2,1)S(1)}, bf16[256,512]{1,0:T(8,128)(2,1)S(1)}, u32[]{:S(2)}, u32[]{:S(2)}) collective-permute-start(bf16[256,512]{1,0:T(8,128)(2,1)S(1)} %collective-permute-done.1.refs_1_), channel_id=1, source_target_pairs={{0,2},{1,3},{2,4},{3,5},{4,6},{5,7},{6,8},{7,9},{8,10},{9,11},{10,... | collective-permute-start | bytes 786440 | tf_op jit(solution)/shard_map/ppermute | solution.py:146
  61.9 11.6 %collective-permute-start.6 = (bf16[256,512]{1,0:T(8,128)(2,1)S(1)}, bf16[256,512]{1,0:T(8,128)(2,1)S(1)}, u32[]{:S(2)}, u32[]{:S(2)}) collective-permute-start(bf16[256,512]{1,0:T(8,128)(2,1)S(1)} %collective-permute-done.3.refs_4_), channel_id=1, source_target_pairs={{0,1},{1,0},{2,3},{3,2},{4,5},{5,4},{6,7},{7,6},{8,9},{9,8},{10,11... | collective-permute-start | bytes 786440 | tf_op jit(solution)/shard_map/ppermute | solution.py:169
Sparse Core Ops, SparseCore 0:
  9.5 52.0 all-gather.1

commit v5 on v4

--- a/solution.py
+++ b/solution.py
@@ -13,7 +13,8 @@
 MIB = 2**20
 
 
-EARLY = ((0, 0), (0, 1), (1, 0), (3, 0), (2, 0), (3, 1), (1, 1))
+FIRST = ((0, 0), (0, 1), (1, 0), (3, 0), (2, 0))
+EARLY = FIRST + ((3, 1), (1, 1))
 LATE = ((2, 1),)
 
 
@@ -84,9 +85,23 @@
     )
 
 
-def head_kernel(place, doms, owner, *refs):
-    pieces = refs[: len(EARLY)]
-    integrals, part, blocks, late_picks, late_order, tiles, sem = refs[len(EARLY) :]
+def pick_kernel(place, doms, owner, *refs):
+    pieces, tiles = refs[:-1], refs[-1]
+    k = pieces[0].shape[0] * len(pieces) // tiles.shape[1]
+    n_act = tiles.shape[0] - 1
+    expand(picks_of(FIRST, place, doms, n_act, k), pieces, tiles.at[:n_act])
+    pairs = owner.shape[1]
+    own = owner[pl.ds(place[2], 1), :] - place[2] * pairs
+    own = jnp.transpose(jnp.broadcast_to(own, (pairs, pairs)))
+    order = order_of(EARLY + LATE, own, place, tiles.shape[1] // (len(FIRST) * STRIDE))
+    half = pairs // 2
+    tiles[n_act, :half, :pairs] = order[:half]
+    tiles[n_act, :half, pairs:] = order[half:]
+
+
+def head_kernel(place, doms, first, *refs):
+    n_next = len(EARLY) - len(FIRST)
+    pieces, (integrals, part, blocks, late_picks, late_order, tiles, sem) = refs[:n_next], refs[n_next:]
     n_act, depth, _ = blocks.shape
 
     def fetch(i):
@@ -96,22 +111,24 @@
     for i in range(n_act):
         fetch(i).start()
     pairs = part.shape[0]
-    per_z = tiles.shape[1] // (len(EARLY) * STRIDE)
     k = doms.shape[0] * doms.shape[1] // pairs
-    picks = picks_of(EARLY + LATE, place, doms, n_act, k)
+    picks = picks_of(EARLY[len(FIRST) :] + LATE, place, doms, n_act, k)
     n_late = late_picks.shape[0]
     for n, pick in enumerate(picks[-n_late:]):
         late_picks[n] = pick
     expand(picks[:-n_late], pieces, tiles)
-    own = owner[pl.ds(place[2], 1), :] - place[2] * pairs
-    own = jnp.transpose(jnp.broadcast_to(own, (pairs, pairs)))
-    late_order[...] = order_of(LATE, own, place, per_z)
-    order = order_of(EARLY, own, place, per_z)
-    total = jnp.zeros((tiles.shape[1], part.shape[1]), jnp.float32)
+    slab = first[n_act, : pairs // 2, :]
+    order = jnp.concatenate([slab[:, :pairs], slab[:, pairs:]], axis=0)
+    n_early = pairs - late_order.shape[1]
+    late_order[...] = order[:, n_early:]
+    order = order[:, :n_early]
+    above = jnp.zeros((first.shape[1], part.shape[1]), jnp.float32)
+    below = jnp.zeros((tiles.shape[1], part.shape[1]), jnp.float32)
     for i in range(n_act):
         fetch(i).wait()
-        total = total + jnp.dot(tiles[i], blocks[i], preferred_element_type=jnp.float32)
-    part[...] = reorder(order, total)
+        above = above + jnp.dot(first[i], blocks[i], preferred_element_type=jnp.float32)
+        below = below + jnp.dot(tiles[i], blocks[i], preferred_element_type=jnp.float32)
+    part[...] = reorder(order, jnp.concatenate([above, below], axis=0))
 
 
 def finish_kernel(part, blocks, late_picks, late_order, *refs):
@@ -182,18 +199,25 @@
         jax.ShapeDtypeStruct((n_late // chunk, n_act * chunk, doms.shape[1]), jnp.bfloat16),
         jax.ShapeDtypeStruct((pairs, n_late), jnp.bfloat16),
     )
+    first = early[: len(FIRST)]
+    n_first = sum(p.shape[0] for p in first) // k
+    tiles = pl.pallas_call(
+        pick_kernel,
+        in_specs=[smem] + [vmem] * (2 + len(first)),
+        out_specs=vmem,
+        out_shape=jax.ShapeDtypeStruct((n_act + 1, n_first, depth), jnp.bfloat16),
+        compiler_params=pltpu.CompilerParams(vmem_limit_bytes=8 * MIB),
+        cost_estimate=cost(2**28),
+    )(place, doms, owners, *first)
     prepared = pl.pallas_call(
         head_kernel,
-        in_specs=[smem] + [vmem] * (2 + len(early)) + [pl.BlockSpec(memory_space=pl.ANY)],
+        in_specs=[smem] + [vmem] * (2 + len(early) - len(FIRST)) + [pl.BlockSpec(memory_space=pl.ANY)],
         out_specs=(vmem,) * len(prepared),
         out_shape=prepared,
-        scratch_shapes=[
-            pltpu.VMEM((n_act, n_early, depth), jnp.bfloat16),
-            pltpu.SemaphoreType.DMA((n_act,)),
-        ],
+        scratch_shapes=[pltpu.VMEM((n_act, n_early - n_first, depth), jnp.bfloat16), pltpu.SemaphoreType.DMA((n_act,))],
         compiler_params=pltpu.CompilerParams(vmem_limit_bytes=HEAD_MIB * MIB),
         cost_estimate=cost(2**29),
-    )(place, doms, owners, *early, whole)
+    )(place, doms, tiles, *early[len(FIRST) :], whole)
     return pl.pallas_call(
         finish_kernel,
         in_specs=[vmem] * (len(prepared) + len(late)),

time: 82.4 us -> 81.6 us (level)
  waiting for transfers between devices: 7.95 us -> 6.77 us
    ppermute x5, waiting for transfers between devices: 7.23 us -> 6.06 us  [send(): lax.ppermute(x, 'grp', [(g, (g + hops * HALF_Y) % n_grp) for g in range(n...]
    pallas_call x1 -> x2, Pallas kernels: 4.07 us -> 4.45 us  [the longest x1 3.28 us: on_device(): pl.pallas_call(head_kernel, in_specs=[smem] + [vmem] * (2 + len(early) -...]
where the time goes in v5:
time: 81.6 us; the launch traced here: 81.1 us
  blocking collectives  27.1 us (33%)
  starting transfers between devices  25.4 us (31%)
  between operations  13.6 us (17%)
  waiting for transfers between devices  6.77 us (8%)
  Pallas kernels  5.97 us (7%)
  local copies, waits for them, and re-layouts  1.14 us (1%)
  other arithmetic  1.12 us (1%)
    all_gather x1, blocking collectives, on_device(): lax.all_gather(amps, 'grp', axis=0, tiled=True, axis_index_groups=strided)  27.1 us
    ppermute x5, starting transfers between devices, send(): lax.ppermute(x, 'grp', [(g, (g + hops * HALF_Y) % n_grp) for g in range(n...  18.1 us
    ppermute x5, waiting for transfers between devices, send(): lax.ppermute(x, 'grp', [(g, (g + hops * HALF_Y) % n_grp) for g in range(n...  6.06 us
    ppermute x1, starting transfers between devices, on_device(): near_x = lax.ppermute(near, 'grp', [(g, g ^ 1) for g in range(n_grp)])  5.09 us
    pallas_call x1, Pallas kernels, on_device(): pl.pallas_call(head_kernel, in_specs=[smem] + [vmem] * (2 + len(early) -...  3.28 us
    ppermute x1, starting transfers between devices, on_device(): far_x = lax.ppermute(far, 'grp', [(g, g ^ 1) for g in range(n_grp)])  2.24 us
  transfers between devices with their start and end apart: 8, of which 2 were waited for; matrix products, arithmetic and copies ran while one was open for 3% of the time, Pallas kernels for 5%

profile of v5, /device:TPU:6, one launch (start us, length us, event | category | flops | bytes accessed | tf_op | source)
XLA Modules:
  0.0 81.1 jit_solution(15366496194469746272)
XLA Ops:
  6.5 0.0 copy-start
  6.5 0.0 all-gather.2.cloned.1.call-start
  6.5 0.7 all-gather.2.cloned.1.call-update
  7.3 27.1 %all_gather.6 = bf16[32,8,512]{2,1,0:T(8,128)(2,1)S(1)} all-gather(bf16[8,8,512]{2,1,0:T(8,128)(2,1)} %param.5), channel_id=1, replica_groups={{0,8,16,24},{1,9,17,25},{2,10,18,26},{3,11,19,27},{4,12,20,28},{5,13,21..., dimensions={0}, use_global_device_ids=true | all-gather | bytes 327680 | tf_op jit(solution)/shard_map/all_gather | solution.py:165
  34.4 5.1 %collective-permute-start.1 = (bf16[256,512]{1,0:T(8,128)(2,1)S(1)}, bf16[256,512]{1,0:T(8,128)(2,1)S(1)}, u32[]{:S(2)}, u32[]{:S(2)}) collective-permute-start(bf16[256,512]{1,0:T(8,128)(2,1)S(1)} %bitcast.6), channel_id=1, source_target_pairs={{0,1},{1,0},{2,3},{3,2},{4,5},{5,4},{6,7},{7,6},{8,9},{9,8},{10,11... | collective-permute-start | bytes 786440 | tf_op jit(solution)/shard_map/ppermute | solution.py:167
  39.5 4.0 %collective-permute-start = (bf16[256,512]{1,0:T(8,128)(2,1)S(1)}, bf16[256,512]{1,0:T(8,128)(2,1)S(1)}, u32[]{:S(2)}, u32[]{:S(2)}) collective-permute-start(bf16[256,512]{1,0:T(8,128)(2,1)S(1)} %bitcast.7), channel_id=1, source_target_pairs={{0,30},{1,31},{2,0},{3,1},{4,2},{5,3},{6,4},{7,5},{8,6},{9,7},{10,... | collective-permute-start | bytes 786440 | tf_op jit(solution)/shard_map/ppermute | solution.py:163
  43.5 0.9 %fusion = pred[16]{0:T(512)(128)(4,1)S(1)} fusion(s32[16,16]{1,0:T(8,128)} %param.8, s32[]{:T(128)S(6)} %select_n.29), kind=kLoop, calls=%fused_computation.3 | loop fusion | flops 16 | bytes 84 | tf_op jit(solution)/shard_map/gt | solution.py:171
  44.4 0.1 convert_reduce_fusion
  44.5 0.0 copy-done
  44.5 0.1 select_reduce_fusion
  44.6 0.7 reshape.23.owner
  45.4 0.1 copy.10
  45.5 0.1 reshape.21
  45.6 0.1 reshape.22.doms
  45.7 0.1 concatenate.3.place
  45.8 2.0 %collective-permute-done.refs_2_ = bf16[256,512]{1,0:T(8,128)(2,1)S(1)} collective-permute-done((bf16[256,512]{1,0:T(8,128)(2,1)S(1)}, bf16[256,512]{1,0:T(8,128)(2,1)S(1)}, u32[]{:S(2)}, u32[]{:S(2)}) %collective-permute-start) | collective-permute-done | bytes 262176 | tf_op jit(solution)/shard_map/ppermute | solution.py:163
  47.7 5.2 %collective-permute-start.3 = (bf16[256,512]{1,0:T(8,128)(2,1)S(1)}, bf16[256,512]{1,0:T(8,128)(2,1)S(1)}, u32[]{:S(2)}, u32[]{:S(2)}) collective-permute-start(bf16[256,512]{1,0:T(8,128)(2,1)S(1)} %collective-permute-done.refs_2_), channel_id=1, source_target_pairs={{0,30},{1,31},{2,0},{3,1},{4,2},{5,3},{6,4},{7,5},{8,6},{9,7},{10,... | collective-permute-start | bytes 786440 | tf_op jit(solution)/shard_map/ppermute | solution.py:163
  52.9 1.9 %collective-permute-start.2 = (bf16[256,512]{1,0:T(8,128)(2,1)S(1)}, bf16[256,512]{1,0:T(8,128)(2,1)S(1)}, u32[]{:S(2)}, u32[]{:S(2)}) collective-permute-start(bf16[256,512]{1,0:T(8,128)(2,1)S(1)} %bitcast.8), channel_id=1, source_target_pairs={{0,2},{1,3},{2,4},{3,5},{4,6},{5,7},{6,8},{7,9},{8,10},{9,11},{10,... | collective-permute-start | bytes 786440 | tf_op jit(solution)/shard_map/ppermute | solution.py:163
  54.8 0.0 collective-permute-done.1.refs_1_
  54.8 5.1 %collective-permute-start.5 = (bf16[256,512]{1,0:T(8,128)(2,1)S(1)}, bf16[256,512]{1,0:T(8,128)(2,1)S(1)}, u32[]{:S(2)}, u32[]{:S(2)}) collective-permute-start(bf16[256,512]{1,0:T(8,128)(2,1)S(1)} %collective-permute-done.1.refs_1_), channel_id=1, source_target_pairs={{0,30},{1,31},{2,0},{3,1},{4,2},{5,3},{6,4},{7,5},{8,6},{9,7},{10,... | collective-permute-start | bytes 786440 | tf_op jit(solution)/shard_map/ppermute | solution.py:163
  60.0 1.9 %collective-permute-start.4 = (bf16[256,512]{1,0:T(8,128)(2,1)S(1)}, bf16[256,512]{1,0:T(8,128)(2,1)S(1)}, u32[]{:S(2)}, u32[]{:S(2)}) collective-permute-start(bf16[256,512]{1,0:T(8,128)(2,1)S(1)} %collective-permute-done.1.refs_1_), channel_id=1, source_target_pairs={{0,2},{1,3},{2,4},{3,5},{4,6},{5,7},{6,8},{7,9},{8,10},{9,11},{10,... | collective-permute-start | bytes 786440 | tf_op jit(solution)/shard_map/ppermute | solution.py:163
  61.9 0.0 collective-permute-done.3.refs_4_
  61.9 2.2 %collective-permute-start.6 = (bf16[256,512]{1,0:T(8,128)(2,1)S(1)}, bf16[256,512]{1,0:T(8,128)(2,1)S(1)}, u32[]{:S(2)}, u32[]{:S(2)}) collective-permute-start(bf16[256,512]{1,0:T(8,128)(2,1)S(1)} %collective-permute-done.3.refs_4_), channel_id=1, source_target_pairs={{0,1},{1,0},{2,3},{3,2},{4,5},{5,4},{6,7},{7,6},{8,9},{9,8},{10,11... | collective-permute-start | bytes 786440 | tf_op jit(solution)/shard_map/ppermute | solution.py:186
  64.2 0.0 collective-permute-done.2.refs_3_
  64.2 1.2 %shard_map.55.first = bf16[9,160,512]{2,1,0:T(8,128)(2,1)S(1)} custom-call(s32[12]{0:T(128)S(1)} %concatenate.3.place, s32[16,128]{1,0:T(8,128)S(1)} %reshape.22.doms, s32[16,256]{1,0:T(8,128)S(1)} %reshape.23.owner, bf16[256,512]{1,0:T(8,128)(2,1)S(1)} %bitcast.9, bf16[256,512]{1,0:T(8,128)(2,1)S(1)} %collective-permute-done.1.refs_1_, ...), custom_call_target="tpu_custom_call" | custom-call | flops 268435456 | bytes 2097152 | tf_op jit(solution)/shard_map/pallas_call | solution.py:204
  65.4 0.0 collective-permute-done.5.refs_1_
  65.4 4.1 %collective-permute-done.4.refs_0_ = bf16[256,512]{1,0:T(8,128)(2,1)S(1)} collective-permute-done((bf16[256,512]{1,0:T(8,128)(2,1)S(1)}, bf16[256,512]{1,0:T(8,128)(2,1)S(1)}, u32[]{:S(2)}, u32[]{:S(2)}) %collective-permute-start.4) | collective-permute-done | bytes 262176 | tf_op jit(solution)/shard_map/ppermute | solution.py:163
  69.5 0.0 all-gather.2.cloned.1.call-done.refs_2_
  69.5 3.3 %shard_map.56 = (f32[256,256]{1,0:T(8,128)S(1)}, bf16[8,512,256]{2,1,0:T(8,128)(2,1)S(1)}, bf16[2,128,128]{2,1,0:T(8,128)(2,1)S(1)}, bf16[256,32]{1,0:T(8,128)(2,1)S(1)}) custom-call(s32[12]{0:T(128)S(1)} %concatenate.3.place, s32[16,128]{1,0:T(8,128)S(1)} %reshape.22.doms, bf16[9,160,512]{2,1,0:T(8,128)(2,1)S(1)} %shard_map.55.first, ...), custom_call_target="tpu_custom_call" | custom-call | flops 536870912 | bytes 2097152 | tf_op jit(solution)/shard_map/pallas_call | solution.py:212
  72.8 0.0 collective-permute-done.6.refs_0_
  72.8 1.5 %shard_map.57 = f32[256,256]{1,0:T(8,128)} custom-call(f32[256,256]{1,0:T(8,128)S(1)} %get-tuple-element.17.part, bf16[8,512,256]{2,1,0:T(8,128)(2,1)S(1)} %get-tuple-element.18.blocks, bf16[2,128,128]{2,1,0:T(8,128)(2,1)S(1)} %get-tuple-element.19.late_picks, bf16[256,32]{1,0:T(8,128)(2,1)S(1)} %get-tuple-element.20.late_order, ...), custom_call_target="tpu_custom_call" | custom-call | flops 134217728 | bytes 2097152 | tf_op jit(solution)/shard_map/pallas_call | solution.py:221
  (2 shorter events, 0.0 us)
Async XLA Ops:
  6.5 37.9 %copy-start = (s32[4096,8]{0,1:T(8,128)S(1)}, s32[4096,8]{0,1:T(8,128)}, u32[]{:S(2)}) copy-start(s32[4096,8]{0,1:T(8,128)} %param.6) | copy-start | bytes 393220
  6.5 62.9 %all-gather.2.cloned.1.call-start = ((), (), s32[]{:S(2)}) async-start(), calls=%async_computation | async-start | bytes 4456448 | tf_op jit(solution)/shard_map/all_gather | solution.py:154
  34.4 20.5 %collective-permute-start.1 = (bf16[256,512]{1,0:T(8,128)(2,1)S(1)}, bf16[256,512]{1,0:T(8,128)(2,1)S(1)}, u32[]{:S(2)}, u32[]{:S(2)}) collective-permute-start(bf16[256,512]{1,0:T(8,128)(2,1)S(1)} %bitcast.6), channel_id=1, source_target_pairs={{0,1},{1,0},{2,3},{3,2},{4,5},{5,4},{6,7},{7,6},{8,9},{9,8},{10,11... | collective-permute-start | bytes 786440 | tf_op jit(solution)/shard_map/ppermute | solution.py:167
  39.5 8.3 %collective-permute-start = (bf16[256,512]{1,0:T(8,128)(2,1)S(1)}, bf16[256,512]{1,0:T(8,128)(2,1)S(1)}, u32[]{:S(2)}, u32[]{:S(2)}) collective-permute-start(bf16[256,512]{1,0:T(8,128)(2,1)S(1)} %bitcast.7), channel_id=1, source_target_pairs={{0,30},{1,31},{2,0},{3,1},{4,2},{5,3},{6,4},{7,5},{8,6},{9,7},{10,... | collective-permute-start | bytes 786440 | tf_op jit(solution)/shard_map/ppermute | solution.py:163
  47.7 14.2 %collective-permute-start.3 = (bf16[256,512]{1,0:T(8,128)(2,1)S(1)}, bf16[256,512]{1,0:T(8,128)(2,1)S(1)}, u32[]{:S(2)}, u32[]{:S(2)}) collective-permute-start(bf16[256,512]{1,0:T(8,128)(2,1)S(1)} %collective-permute-done.refs_2_), channel_id=1, source_target_pairs={{0,30},{1,31},{2,0},{3,1},{4,2},{5,3},{6,4},{7,5},{8,6},{9,7},{10,... | collective-permute-start | bytes 786440 | tf_op jit(solution)/shard_map/ppermute | solution.py:163
  52.9 11.3 %collective-permute-start.2 = (bf16[256,512]{1,0:T(8,128)(2,1)S(1)}, bf16[256,512]{1,0:T(8,128)(2,1)S(1)}, u32[]{:S(2)}, u32[]{:S(2)}) collective-permute-start(bf16[256,512]{1,0:T(8,128)(2,1)S(1)} %bitcast.8), channel_id=1, source_target_pairs={{0,2},{1,3},{2,4},{3,5},{4,6},{5,7},{6,8},{7,9},{8,10},{9,11},{10,... | collective-permute-start | bytes 786440 | tf_op jit(solution)/shard_map/ppermute | solution.py:163
  54.8 10.5 %collective-permute-start.5 = (bf16[256,512]{1,0:T(8,128)(2,1)S(1)}, bf16[256,512]{1,0:T(8,128)(2,1)S(1)}, u32[]{:S(2)}, u32[]{:S(2)}) collective-permute-start(bf16[256,512]{1,0:T(8,128)(2,1)S(1)} %collective-permute-done.1.refs_1_), channel_id=1, source_target_pairs={{0,30},{1,31},{2,0},{3,1},{4,2},{5,3},{6,4},{7,5},{8,6},{9,7},{10,... | collective-permute-start | bytes 786440 | tf_op jit(solution)/shard_map/ppermute | solution.py:163
  60.0 9.5 %collective-permute-start.4 = (bf16[256,512]{1,0:T(8,128)(2,1)S(1)}, bf16[256,512]{1,0:T(8,128)(2,1)S(1)}, u32[]{:S(2)}, u32[]{:S(2)}) collective-permute-start(bf16[256,512]{1,0:T(8,128)(2,1)S(1)} %collective-permute-done.1.refs_1_), channel_id=1, source_target_pairs={{0,2},{1,3},{2,4},{3,5},{4,6},{5,7},{6,8},{7,9},{8,10},{9,11},{10,... | collective-permute-start | bytes 786440 | tf_op jit(solution)/shard_map/ppermute | solution.py:163
  61.9 10.8 %collective-permute-start.6 = (bf16[256,512]{1,0:T(8,128)(2,1)S(1)}, bf16[256,512]{1,0:T(8,128)(2,1)S(1)}, u32[]{:S(2)}, u32[]{:S(2)}) collective-permute-start(bf16[256,512]{1,0:T(8,128)(2,1)S(1)} %collective-permute-done.3.refs_4_), channel_id=1, source_target_pairs={{0,1},{1,0},{2,3},{3,2},{4,5},{5,4},{6,7},{7,6},{8,9},{9,8},{10,11... | collective-permute-start | bytes 786440 | tf_op jit(solution)/shard_map/ppermute | solution.py:186
Sparse Core Ops, SparseCore 0:
  9.5 52.0 all-gather.1
